TPU v7x, 32 devices: a whole 2x2x4 slice. The times are simulated.
32 devices in a mesh: dp: 8 (over z, core), ctx: 4 (over y, x).
Axes of the slice: x: 2, y: 2, z: 4, core: 2. Of those that a mesh axis runs over, the one named last changes fastest.
Arguments:
- inputs: float32 [8, 512, 1024], P('dp', 'ctx'), may hold values from -6 to 6
- segments: int32 [8, 512], P('dp'), may hold values from 0 to 7, never falling along the last dimension, each value on 1 to 256 neighbouring positions
- cotangent: float32 [8, 512, 1024], P('dp', 'ctx'), may hold values from -6 to 6
- mixer_params: float32 [8192, 1024], P(('dp', 'ctx')), may hold values from -0.1875 to 0.1875
- mixer_first: float32 [8192, 1024], P(('dp', 'ctx')), may hold values from -12 to 12
- mixer_second: float32 [8192, 1024], P(('dp', 'ctx')), may hold values from 10 to 1000
- feed_params: float32 [8448, 1024], P(('dp', 'ctx')), may hold values from -0.1875 to 0.1875
- feed_first: float32 [8448, 1024], P(('dp', 'ctx')), may hold values from -12 to 12
- feed_second: float32 [8448, 1024], P(('dp', 'ctx')), may hold values from 10 to 1000
- small_params: float32 [35088], replicated, may hold values from -8 to 1.5
- small_first: float32 [35088], replicated, may hold values from -12 to 12
- small_second: float32 [35088], replicated, may hold values from 10 to 1000
Outputs:
- output: float32 [8, 512, 1024], P('dp', 'ctx')
- input_grad: float32 [8, 512, 1024], P('dp', 'ctx')
- mixer_grad: float32 [8192, 1024], P(('dp', 'ctx'))
- feed_grad: float32 [8448, 1024], P(('dp', 'ctx'))
- small_grad: float32 [35088], replicated
- mixer_new: float32 [8192, 1024], P(('dp', 'ctx'))
- mixer_moment: float32 [8192, 1024], P(('dp', 'ctx'))
- mixer_square: float32 [8192, 1024], P(('dp', 'ctx'))
- feed_new: float32 [8448, 1024], P(('dp', 'ctx'))
- feed_moment: float32 [8448, 1024], P(('dp', 'ctx'))
- feed_square: float32 [8448, 1024], P(('dp', 'ctx'))
- small_new: float32 [35088], replicated
- small_moment: float32 [35088], replicated
- small_square: float32 [35088], replicated
Inputs may be any that keep to these rules, and one draw needn't show every extreme that they name: `segments`: segment numbers never fall along a sequence; a segment holds 1 to 256 tokens and in each sequence one holds exactly 256.
All inputs are finite; a program needn't handle non-finite values.
Results may differ from a plain program's by a relative error of at most 0.022.
Values may be sent and summed in bfloat16 or wider, within the bound.
A program may use at most 256 MiB of HBM per device.

v0:
```python
import jax
import jax.numpy as jnp
from jax import lax
from jax.experimental import pallas as pl
from jax.experimental.pallas import tpu as pltpu
from jax.sharding import PartitionSpec as P

D = 1024
H = 8
DK = 128
DV = 256
FF = 2816
CONV = 4
SPAN = 128
GROUP = 4
STEP = 10


PRECISE = lax.Precision.HIGHEST
CORE = lax.Precision.DEFAULT
EPS_NORM = 1e-06
EPS_GATE = 1e-05
EPS_KEYS = 1e-06
LEARN_RATE = 0.002
FIRST_RATE = 0.9
SECOND_RATE = 0.95
EPS_ADAM = 1e-08
WEIGHT_DECAY = 0.1


def passed_along(shard, axis, by):
    count = lax.axis_size(axis)
    pairs = [(i, i + by) for i in range(count) if 0 <= i + by < count]
    return lax.ppermute(shard, axis, pairs)


def dot(left, right, contract=((1,), (0,)), precision=None):
    return lax.dot_general(
        left, right, (contract, ((), ())), precision=precision, preferred_element_type=jnp.float32
    )


def unit_rows(raw, scale):
    inverse = lax.rsqrt(jnp.sum(raw * raw, axis=-1, keepdims=True) + EPS_KEYS)
    return (raw * (inverse * scale), inverse)


def unit_back(raw, inverse, scale, upstream):
    upstream = upstream * scale
    shared = jnp.sum(raw * upstream, axis=-1, keepdims=True)
    return inverse * upstream - raw * (inverse * inverse * inverse * shared)


def block_decays(rows, columns, extent):
    places = lax.broadcasted_iota(jnp.int32, (extent, extent), 0)
    others = lax.broadcasted_iota(jnp.int32, (extent, extent), 1)
    keep = (columns[:, 2:3] == rows[2:3, :]) & (places >= others)
    spread = jnp.minimum(columns[:, 1:2] - rows[1:2, :], 0.0)
    return (jnp.where(keep, jnp.exp(spread), 0.0), places, others)


def block_kernel(
    q_ref, k_ref, v_ref, row_ref, column_ref,
    inverse_ref, w_ref, u_ref, r_ref, o_ref, transfer_ref, offset_ref,
):
    group = row_ref.shape[0]
    extent = q_ref.shape[0]
    systems, solved, pieces = ([], [], [])
    for h in range(group):
        rows, columns = (row_ref[h, 0], column_ref[h, 0])
        keys = slice(h * DK, (h + 1) * DK)
        queries, _ = unit_rows(q_ref[:, keys], DK ** (-0.5))
        key_rows, _ = unit_rows(k_ref[:, keys], 1.0)
        decays, places, others = block_decays(rows, columns, extent)
        weighted = decays * rows[0:1, :]
        key_key = dot(key_rows, key_rows, ((1,), (1,)), CORE)
        system = jnp.where(places > others, weighted * key_key, 0.0)
        apart = places ^ others
        systems.append(system)
        solved.append(
            jnp.where(places == others, 1.0, 0.0) - jnp.where(apart < 2, system, 0.0)
        )
        mixing = weighted * dot(queries, key_rows, ((1,), (1,)), CORE)
        pieces.append((queries, key_rows, mixing, columns))
    size = 2
    while size < extent:
        level = (apart >= size) & (apart < 2 * size)
        halves = [
            dot(solved[h], jnp.where(level, systems[h], 0.0), precision=PRECISE)
            for h in range(group)
        ]
        solved = [
            solved[h] - dot(halves[h], solved[h], precision=PRECISE) for h in range(group)
        ]
        size = 2 * size
    for h in range(group):
        queries, key_rows, mixing, columns = pieces[h]
        keys = slice(h * DK, (h + 1) * DK)
        values = slice(h * DV, (h + 1) * DV)
        carried = columns[:, 3:4]
        inverse_ref[0, h] = solved[h]
        w_part = dot(solved[h], carried * key_rows, precision=CORE)
        u_part = dot(solved[h], v_ref[:, values], precision=CORE)
        w_ref[:, keys] = w_part
        u_ref[:, values] = u_part
        r_ref[:, keys] = carried * queries - dot(mixing, w_part, precision=CORE)
        o_ref[:, values] = dot(mixing, u_part, precision=CORE)
        last_keys = key_rows * columns[:, 4:5]
        rank = lax.broadcasted_iota(jnp.int32, (DK, DK), 0)
        file = lax.broadcasted_iota(jnp.int32, (DK, DK), 1)
        transfer_ref[0, h] = jnp.where(
            rank == file, carried[extent - 1 : extent, :], 0.0
        ) - dot(last_keys, w_part, ((0,), (0,)), CORE)
        offset_ref[0, h] = dot(last_keys, u_part, ((0,), (0,)), CORE)


def output_kernel(r_ref, o_ref, state_ref, gate_ref, gain_ref, recurrent_ref, mix_ref):
    for h in range(state_ref.shape[1]):
        keys = slice(h * DK, (h + 1) * DK)
        values = slice(h * DV, (h + 1) * DV)
        recurrent = o_ref[:, values] + dot(r_ref[:, keys], state_ref[0, h], precision=CORE)
        recurrent_ref[:, values] = recurrent
        inverse = lax.rsqrt(jnp.mean(recurrent * recurrent, axis=-1, keepdims=True) + EPS_GATE)
        mix_ref[:, values] = (
            recurrent * inverse * gain_ref[...] * jax.nn.silu(gate_ref[:, values])
        ).astype(jnp.bfloat16)


def gate_back_kernel(
    mix_ref, recurrent_ref, gate_ref, gain_ref, r_ref,
    grad_ref, grad_gate_ref, grad_gain_ref, local_ref,
):
    total = jnp.zeros((1, DV), jnp.float32)
    for h in range(local_ref.shape[1]):
        keys = slice(h * DK, (h + 1) * DK)
        values = slice(h * DV, (h + 1) * DV)
        upstream, recurrent, gate = (mix_ref[:, values], recurrent_ref[:, values], gate_ref[:, values])
        inverse = lax.rsqrt(jnp.mean(recurrent * recurrent, axis=-1, keepdims=True) + EPS_GATE)
        normal = recurrent * inverse
        sig = jax.nn.sigmoid(gate)
        gain = gain_ref[...]
        grad_gate_ref[:, values] = upstream * normal * gain * (sig + gate * sig * (1.0 - sig))
        scaled = upstream * (gate * sig)
        total = total + jnp.sum(scaled * normal, axis=0, keepdims=True)
        scaled = scaled * gain
        grad = inverse * (scaled - normal * jnp.mean(scaled * normal, axis=-1, keepdims=True))
        grad_ref[:, values] = grad
        local_ref[0, h] = dot(r_ref[:, keys], grad, ((0,), (0,)), CORE)
    grad_gain_ref[0] = total


def block_back_kernel(
    q_ref, k_ref, v_ref, row_ref, column_ref, inverse_ref, w_ref, u_ref, state_ref, grad_ref, next_ref,
    grad_q_ref, grad_k_ref, grad_v_ref, grad_row_ref, grad_column_ref,
):
    group = row_ref.shape[0]
    extent = q_ref.shape[0]
    for h in range(group):
        rows, columns = (row_ref[h, 0], column_ref[h, 0])
        keys = slice(h * DK, (h + 1) * DK)
        values = slice(h * DV, (h + 1) * DV)
        raw_q, raw_k = (q_ref[:, keys], k_ref[:, keys])
        queries, inverse_q = unit_rows(raw_q, DK ** (-0.5))
        key_rows, inverse_k = unit_rows(raw_k, 1.0)
        decays, places, others = block_decays(rows, columns, extent)
        beta = rows[0:1, :]
        carried, last = (columns[:, 3:4], columns[:, 4:5])
        weighted = decays * beta
        strict = places > others
        key_key = dot(key_rows, key_rows, ((1,), (1,)), CORE)
        query_key = dot(queries, key_rows, ((1,), (1,)), CORE)
        state, upstream, after = (state_ref[0, h], grad_ref[:, values], next_ref[0, h])
        delta = u_ref[:, values] - dot(w_ref[:, keys], state, precision=CORE)
        grad_delta = dot(weighted * query_key, upstream, ((0,), (0,)), CORE) + dot(
            key_rows * last, after, precision=CORE
        )
        grad_mixing = dot(upstream, delta, ((1,), (1,)), CORE)
        grad_target = dot(inverse_ref[0, h], grad_delta, ((0,), (0,)), CORE)
        grad_system = jnp.where(strict, -dot(grad_target, delta, ((1,), (1,)), CORE), 0.0)
        up_state = dot(upstream, state, ((1,), (1,)), CORE)
        down_state = dot(grad_target, state, ((1,), (1,)), CORE)
        grad_last = dot(delta, after, ((1,), (1,)), CORE)
        grad_carried = jnp.sum(up_state * queries - down_state * key_rows, axis=-1, keepdims=True)
        line = lax.broadcasted_iota(jnp.int32, (extent, 1), 0)
        grad_carried = grad_carried + jnp.where(
            line == extent - 1, jnp.sum(after * state, keepdims=True), 0.0
        )
        grad_qk = grad_mixing * weighted
        grad_kk = grad_system * weighted
        grad_queries = carried * up_state + dot(grad_qk, key_rows, precision=CORE)
        grad_keys = (
            grad_last * last
            - carried * down_state
            + dot(grad_qk, queries, ((0,), (0,)), CORE)
            + dot(grad_kk, key_rows, precision=CORE)
            + dot(grad_kk, key_rows, ((0,), (0,)), CORE)
        )
        grad_q_ref[:, keys] = unit_back(raw_q, inverse_q, DK ** (-0.5), grad_queries)
        grad_k_ref[:, keys] = unit_back(raw_k, inverse_k, 1.0, grad_keys)
        grad_v_ref[:, values] = grad_target
        spread = (grad_system * key_key + grad_mixing * query_key) * decays
        grad_row_ref[h, 0] = jnp.zeros_like(rows)
        grad_row_ref[h, 0, 0:1, :] = jnp.sum(spread, axis=0, keepdims=True)
        grad_row_ref[h, 0, 1:2, :] = -jnp.sum(spread * beta, axis=0, keepdims=True)
        place = lax.broadcasted_iota(jnp.int32, (extent, 8), 1)
        grad_column_ref[h, 0] = jnp.where(
            place == 1,
            jnp.sum(spread * beta, axis=-1, keepdims=True),
            jnp.where(
                place == 3,
                grad_carried,
                jnp.where(
                    place == 4, jnp.sum(grad_last * key_rows, axis=-1, keepdims=True), 0.0
                ),
            ),
        )


def block_scalars(beta_logit, alpha_logit, decay_log, decay_bias, segment_ids, segment_before, span):
    token_count = beta_logit.shape[0]
    count = token_count // span
    beta = jax.nn.sigmoid(beta_logit)
    log_decay = -jnp.exp(decay_log) * jax.nn.softplus(alpha_logit + decay_bias)

    def blocks(tensor):
        return tensor.T.reshape(H, count, span)

    beta, log_decay = (blocks(beta), blocks(log_decay))
    segment_blocks = segment_ids.reshape(count, span)
    befores = jnp.concatenate([jnp.reshape(segment_before, (1,)), segment_blocks[:-1, -1]])
    upper = (jnp.arange(span)[:, None] <= jnp.arange(span)[None, :]).astype(jnp.float32)
    running = jnp.einsum("hcs,st->hct", log_decay, upper, precision=PRECISE)
    carried = jnp.where((segment_blocks == befores[:, None])[None], jnp.exp(running), 0.0)
    ending = (segment_blocks == segment_blocks[:, -1:])[None]
    last = jnp.where(ending, jnp.exp(jnp.minimum(running[:, :, -1:] - running, 0.0)), 0.0) * beta
    return (beta, running, carried, last)


def kernel_call(body, grid, args, in_specs, outs, out_specs):
    return pl.pallas_call(
        body,
        grid=grid,
        in_specs=in_specs,
        out_specs=out_specs,
        out_shape=[jax.ShapeDtypeStruct(shape, dtype) for shape, dtype in outs],
        compiler_params=pltpu.CompilerParams(vmem_limit_bytes=48 * 1024 * 1024),
    )(*args)


def active_rows(extended, conv_weight, segment_wide):
    margin = CONV - 1
    token_count = extended.shape[0] - margin
    segment_ids = segment_wide[margin:]
    mixed = jnp.zeros((token_count, extended.shape[1]), extended.dtype)
    for offset in range(CONV):
        start_row = margin - offset
        window = extended[start_row : start_row + token_count]
        keep_mask = (segment_wide[start_row : start_row + token_count] == segment_ids)[:, None]
        mixed = mixed + jnp.where(keep_mask, window * conv_weight[offset], 0.0)
    return jax.nn.silu(mixed)


def norm_back(values, inverse, gain_row, upstream):
    weighted = gain_row * upstream
    return inverse * weighted - values * inverse**3 * jnp.mean(
        weighted * values, axis=-1, keepdims=True
    )


def unpack_small(packed):
    channels = 2 * H * DK + H * DV
    bounds = [CONV * channels, D, D, DV, 2 * H * D, H, H]
    pieces = []
    cursor = 0
    for extent in bounds:
        pieces.append(packed[cursor : cursor + extent])
        cursor = cursor + extent
    return (
        pieces[0].reshape(CONV, channels),
        pieces[1],
        pieces[2],
        pieces[3],
        pieces[4].reshape(2 * H, D),
        pieces[5],
        pieces[6],
    )


def adamw(current, gradient, moment, square):
    moment = FIRST_RATE * moment + (1.0 - FIRST_RATE) * gradient
    square = SECOND_RATE * square + (1.0 - SECOND_RATE) * gradient * gradient
    update = (
        moment
        / (1.0 - FIRST_RATE**STEP)
        / (jnp.sqrt(square / (1.0 - SECOND_RATE**STEP)) + EPS_ADAM)
    )
    return (current - LEARN_RATE * (update + WEIGHT_DECAY * current), moment, square)


def owner_rows(first_left, first_right, second_left, second_right):
    def product(left_part, right_part):
        return jnp.einsum(
            "tr,td->rd", left_part, right_part, preferred_element_type=jnp.float32
        ).astype(jnp.bfloat16)

    return jnp.concatenate(
        [product(first_left, first_right), product(second_left, second_right)], axis=0
    )


def to_owners(rows):
    return lax.psum_scatter(rows, ("dp", "ctx"), scatter_dimension=0, tiled=True).astype(
        jnp.float32
    )


def shifted(shard, by):
    return passed_along(shard, "ctx", by)


def per_device(
    inputs,
    segments,
    cotangent,
    mixer_params,
    mixer_first,
    mixer_second,
    feed_params,
    feed_first,
    feed_second,
    small_params,
    small_first,
    small_second,
):
    mixer_weights = lax.all_gather(
        mixer_params.astype(jnp.bfloat16), ("dp", "ctx"), axis=0, tiled=True
    )
    feed_half, mixer_weights = lax.optimization_barrier(
        (feed_params.astype(jnp.bfloat16), mixer_weights)
    )
    feed_weights = lax.all_gather(feed_half, ("dp", "ctx"), axis=0, tiled=True)
    conv_weight, gain_first, gain_second, out_gain, gate_rows, decay_log, decay_bias = unpack_small(
        small_params
    )
    channels = 2 * H * DK + H * DV
    input_rows = channels + H * DV
    margin = CONV - 1
    in_weight = mixer_weights[:input_rows]
    out_weight = mixer_weights[input_rows:]
    up_weight = feed_weights[: 2 * FF]
    down_weight = feed_weights[2 * FF :]
    tokens_here = inputs[0]
    cotangent_here = cotangent[0]
    token_count = tokens_here.shape[0]
    position = lax.axis_index("ctx") * token_count
    segment_padded = jnp.concatenate([jnp.full((margin,), -1, jnp.int32), segments[0]])
    segment_wide = lax.dynamic_slice_in_dim(segment_padded, position, token_count + margin)
    segment_ids = segment_wide[margin:]
    segment_before = segment_wide[margin - 1]
    inverse_first = lax.rsqrt(
        jnp.mean(tokens_here * tokens_here, axis=-1, keepdims=True) + EPS_NORM
    )
    normed = (tokens_here * inverse_first * gain_first).astype(jnp.bfloat16)
    gate_half = gate_rows.astype(jnp.bfloat16)
    logits = jnp.einsum("td,rd->tr", normed, gate_half, preferred_element_type=jnp.float32)
    rim_normed = shifted(normed[token_count - margin :], 1)
    projected = jnp.einsum("td,rd->tr", normed, in_weight, preferred_element_type=jnp.float32)
    rim_rows = jnp.einsum(
        "td,rd->tr", rim_normed, in_weight[:channels], preferred_element_type=jnp.float32
    ).astype(jnp.bfloat16)
    conv_input = projected[:, :channels].astype(jnp.bfloat16)
    gate_pre = projected[:, channels:]
    extended = jnp.concatenate([rim_rows, conv_input]).astype(jnp.float32)

    active, active_back = jax.vjp(
        lambda wide, taps: active_rows(wide, taps, segment_wide), extended, conv_weight
    )
    span = min(SPAN, token_count)
    count = token_count // span
    scalars, scalars_back = jax.vjp(
        lambda *args: block_scalars(*args, segment_ids, segment_before, span),
        logits[:, :H],
        logits[:, H:],
        decay_log,
        decay_bias,
    )
    beta, running, carried, last = scalars
    segment_rows = jnp.broadcast_to(
        segment_ids.astype(jnp.float32).reshape(1, count, span), beta.shape
    )
    blank = jnp.zeros_like(beta)
    row_pack = jnp.stack(
        [beta, running, segment_rows, carried, last, blank, blank, blank], axis=2
    )
    column_pack = jnp.swapaxes(row_pack, 2, 3)
    groups = H // GROUP
    key_blocks = H * DK // (GROUP * DK)
    value_start = 2 * H * DK // (GROUP * DV)
    query_spec = pl.BlockSpec((span, GROUP * DK), lambda c, g: (c, g))
    key_spec = pl.BlockSpec((span, GROUP * DK), lambda c, g: (c, g + key_blocks))
    value_spec = pl.BlockSpec((span, GROUP * DV), lambda c, g: (c, g + value_start))
    wide_spec = pl.BlockSpec((span, GROUP * DV), lambda c, g: (c, g))
    row_spec = pl.BlockSpec((GROUP, 1, 8, span), lambda c, g: (g, c, 0, 0))
    column_spec = pl.BlockSpec((GROUP, 1, span, 8), lambda c, g: (g, c, 0, 0))
    inverse_spec = pl.BlockSpec((1, GROUP, span, span), lambda c, g: (c, g, 0, 0))
    square_spec = pl.BlockSpec((1, GROUP, DK, DK), lambda c, g: (c, g, 0, 0))
    state_spec = pl.BlockSpec((1, GROUP, DK, DV), lambda c, g: (c, g, 0, 0))
    gain_spec = pl.BlockSpec((1, DV), lambda c, g: (0, 0))
    key_out = ((token_count, H * DK), jnp.float32)
    value_out = ((token_count, H * DV), jnp.float32)
    state_out = ((count, H, DK, DV), jnp.float32)
    grid = (count, groups)
    inverse, w_part, u_part, r_part, o_part, transfers, offsets = kernel_call(
        block_kernel,
        grid,
        (active, active, active, row_pack, column_pack),
        [query_spec, key_spec, value_spec, row_spec, column_spec],
        [
            ((count, H, span, span), jnp.float32),
            key_out,
            value_out,
            key_out,
            value_out,
            ((count, H, DK, DK), jnp.float32),
            state_out,
        ],
        [inverse_spec, query_spec, wide_spec, query_spec, wide_spec, square_spec, state_spec],
    )

    def advance(left, right):
        return jnp.einsum(
            "hij,hjw->hiw", left, right, precision=CORE, preferred_element_type=jnp.float32
        )

    def advance_back(left, right):
        return jnp.einsum(
            "hji,hjw->hiw", left, right, precision=CORE, preferred_element_type=jnp.float32
        )

    transfer, offset_state = (transfers[0], offsets[0])
    for block in range(1, count):
        transfer = advance(transfers[block], transfer)
        offset_state = advance(transfers[block], offset_state) + offsets[block]
    ring = lax.axis_size("ctx")
    transfer_half = transfer.astype(jnp.bfloat16)
    offset_half = offset_state.astype(jnp.bfloat16)
    befores = [
        (shifted(transfer_half, by), shifted(offset_half, by)) for by in range(1, ring)
    ]
    state_in = jnp.zeros((H, DK, DV), jnp.float32)
    for transfer_there, offset_there in reversed(befores):
        state_in = advance(transfer_there.astype(jnp.float32), state_in) + offset_there
    states = [state_in]
    for block in range(count - 1):
        states.append(advance(transfers[block], states[-1]) + offsets[block])
    states = jnp.stack(states)
    gain_row = out_gain.reshape(1, DV)
    recurrent_out, mix_half = kernel_call(
        output_kernel,
        grid,
        (r_part, o_part, states, gate_pre, gain_row),
        [query_spec, wide_spec, state_spec, wide_spec, gain_spec],
        [value_out, ((token_count, H * DV), jnp.bfloat16)],
        [wide_spec, wide_spec],
    )
    afters = [shifted(transfer_half, -by) for by in range(1, ring)]
    hidden = tokens_here + jnp.dot(mix_half, out_weight, preferred_element_type=jnp.float32)
    inverse_second = lax.rsqrt(jnp.mean(hidden * hidden, axis=-1, keepdims=True) + EPS_NORM)
    hidden_normed = (hidden * inverse_second * gain_second).astype(jnp.bfloat16)
    gate_up = jnp.einsum("td,rd->tr", hidden_normed, up_weight, preferred_element_type=jnp.float32)
    gate_part = gate_up[:, :FF]
    up_part = gate_up[:, FF:]
    middle = (jax.nn.silu(gate_part) * up_part).astype(jnp.bfloat16)
    result = hidden + jnp.dot(middle, down_weight, preferred_element_type=jnp.float32)
    cotangent_half = cotangent_here.astype(jnp.bfloat16)
    grad_middle = jnp.einsum(
        "td,fd->tf", cotangent_half, down_weight, preferred_element_type=jnp.float32
    )
    sigmoid_gate = jax.nn.sigmoid(gate_part)
    grad_gate = (
        grad_middle * up_part * (sigmoid_gate + gate_part * sigmoid_gate * (1.0 - sigmoid_gate))
    )
    grad_up = grad_middle * gate_part * sigmoid_gate
    grad_gate_up = jnp.concatenate([grad_gate, grad_up], axis=1).astype(jnp.bfloat16)
    grad_hidden_normed = jnp.dot(grad_gate_up, up_weight, preferred_element_type=jnp.float32)
    grad_hidden = cotangent_here + norm_back(
        hidden, inverse_second, gain_second, grad_hidden_normed
    )
    grad_gain_second = jnp.sum(grad_hidden_normed * hidden * inverse_second, axis=0)
    grad_hidden_half = grad_hidden.astype(jnp.bfloat16)
    feed_rows = owner_rows(grad_gate_up, hidden_normed, middle, cotangent_half)
    feed_rows, grad_hidden_half = lax.optimization_barrier((feed_rows, grad_hidden_half))
    feed_grad = to_owners(feed_rows)
    grad_mix = jnp.einsum(
        "td,rd->tr", grad_hidden_half, out_weight, preferred_element_type=jnp.float32
    )
    partial_spec = pl.BlockSpec((1, 1, DV), lambda c, g: (c * groups + g, 0, 0))
    grad_recurrent, grad_gate_pre, gain_parts, locals_back = kernel_call(
        gate_back_kernel,
        grid,
        (grad_mix, recurrent_out, gate_pre, gain_row, r_part),
        [wide_spec, wide_spec, wide_spec, gain_spec, query_spec],
        [value_out, value_out, ((count * groups, 1, DV), jnp.float32), state_out],
        [wide_spec, wide_spec, partial_spec, state_spec],
    )
    grad_out_gain = jnp.sum(gain_parts, axis=(0, 1))
    local_part = locals_back[count - 1]
    for block in range(count - 2, -1, -1):
        local_part = advance_back(transfers[block], local_part) + locals_back[block]
    local_half = local_part.astype(jnp.bfloat16)
    local_afters = [shifted(local_half, -by) for by in range(1, ring)]
    state_grad = jnp.zeros((H, DK, DV), jnp.float32)
    for transfer_there, local_there in reversed(list(zip(afters, local_afters))):
        state_grad = advance_back(transfer_there.astype(jnp.float32), state_grad) + local_there
    nexts = [state_grad]
    for block in range(count - 1, 0, -1):
        nexts.append(advance_back(transfers[block], nexts[-1]) + locals_back[block])
    nexts = jnp.stack(nexts[::-1])
    grad_q, grad_k, grad_v, grad_row_pack, grad_column_pack = kernel_call(
        block_back_kernel,
        grid,
        (
            active,
            active,
            active,
            row_pack,
            column_pack,
            inverse,
            w_part,
            u_part,
            states,
            grad_recurrent,
            nexts,
        ),
        [
            query_spec,
            key_spec,
            value_spec,
            row_spec,
            column_spec,
            inverse_spec,
            query_spec,
            wide_spec,
            state_spec,
            wide_spec,
            state_spec,
        ],
        [key_out, key_out, value_out, (row_pack.shape, jnp.float32), (column_pack.shape, jnp.float32)],
        [query_spec, query_spec, wide_spec, row_spec, column_spec],
    )
    grad_pack = grad_row_pack + jnp.swapaxes(grad_column_pack, 2, 3)
    grad_beta_logit, grad_alpha_logit, grad_decay_log, grad_decay_bias = scalars_back(
        (grad_pack[:, :, 0], grad_pack[:, :, 1], grad_pack[:, :, 3], grad_pack[:, :, 4])
    )
    grad_wide, grad_conv = active_back(jnp.concatenate([grad_q, grad_k, grad_v], axis=1))
    back_rim = passed_along(grad_wide[:margin].astype(jnp.bfloat16), "ctx", -1).astype(jnp.float32)
    grad_conv_input = grad_wide[margin:]
    grad_conv_input = jnp.concatenate(
        [
            grad_conv_input[: token_count - margin],
            grad_conv_input[token_count - margin :] + back_rim,
        ]
    )
    grad_projected = jnp.concatenate([grad_conv_input, grad_gate_pre], axis=1).astype(jnp.bfloat16)
    grad_logits = jnp.concatenate([grad_beta_logit, grad_alpha_logit], axis=1).astype(jnp.bfloat16)
    grad_normed = jnp.dot(grad_projected, in_weight, preferred_element_type=jnp.float32)
    grad_normed = grad_normed + jnp.dot(grad_logits, gate_half, preferred_element_type=jnp.float32)
    grad_inputs = grad_hidden + norm_back(tokens_here, inverse_first, gain_first, grad_normed)
    grad_gain_first = jnp.sum(grad_normed * tokens_here * inverse_first, axis=0)
    gate_grad = jnp.einsum("tr,td->rd", grad_logits, normed, preferred_element_type=jnp.float32)
    small_local = jnp.concatenate(
        [
            grad_conv.reshape(-1),
            grad_gain_first,
            grad_gain_second,
            grad_out_gain,
            gate_grad.reshape(-1),
            grad_decay_log,
            grad_decay_bias,
        ]
    )
    small_grad = lax.psum(small_local, ("dp", "ctx"))
    mixer_grad = to_owners(owner_rows(grad_projected, normed, mix_half, grad_hidden_half))
    mixer_new, mixer_moment, mixer_square = adamw(
        mixer_params, mixer_grad, mixer_first, mixer_second
    )
    feed_new, feed_moment, feed_square = adamw(feed_params, feed_grad, feed_first, feed_second)
    small_new, small_moment, small_square = adamw(
        small_params, small_grad, small_first, small_second
    )
    return (
        result[None],
        grad_inputs[None],
        mixer_grad,
        feed_grad,
        small_grad,
        mixer_new,
        mixer_moment,
        mixer_square,
        feed_new,
        feed_moment,
        feed_square,
        small_new,
        small_moment,
        small_square,
    )


def solution(mesh):
    in_specs = (
        P("dp", "ctx", None),
        P("dp", None),
        P("dp", "ctx", None),
        P(("dp", "ctx"), None),
        P(("dp", "ctx"), None),
        P(("dp", "ctx"), None),
        P(("dp", "ctx"), None),
        P(("dp", "ctx"), None),
        P(("dp", "ctx"), None),
        P(),
        P(),
        P(),
    )
    out_specs = (
        P("dp", "ctx", None),
        P("dp", "ctx", None),
        P(("dp", "ctx"), None),
        P(("dp", "ctx"), None),
        P(),
        P(("dp", "ctx"), None),
        P(("dp", "ctx"), None),
        P(("dp", "ctx"), None),
        P(("dp", "ctx"), None),
        P(("dp", "ctx"), None),
        P(("dp", "ctx"), None),
        P(),
        P(),
        P(),
    )
    return jax.shard_map(
        per_device, mesh=mesh, in_specs=in_specs, out_specs=out_specs, check_vma=False
    )
```

profile of v0, /device:TPU:0, one launch (start us, length us, event | category | flops | bytes accessed | tf_op | source)
XLA Modules:
  0.0 1097.5 jit_solution(15780110668080586362)
XLA Ops:
  10.4 118.1 %all-gather.3.cloned.1.call-done = bf16[8192,1024]{1,0:T(8,128)(2,1)} async-done(((bf16[256,1024]{1,0:T(8,128)(2,1)}), bf16[8192,1024]{1,0:T(8,128)(2,1)}) %all-gather.3.cloned.1.call-update) | async-done | bytes 16777232 | tf_op jit(solution)/shard_map/all_gather | solution.py:335
  130.1 3.2 collective-permute-start
  145.3 7.3 fusion.2
  152.8 5.6 fusion.14
  158.8 3.2 fusion.26
  162.0 9.7 shard_map.227
  172.7 2.7 collective-permute-start.5
  183.8 31.4 %collective-permute-done.2 = bf16[8,128,128]{2,1,0:T(8,128)(2,1)S(1)} collective-permute-done((bf16[8,128,128]{2,1,0:T(8,128)(2,1)}, bf16[8,128,128]{2,1,0:T(8,128)(2,1)S(1)}, u32[]{:S(2)}, u32[]{:S(2)}) %collective-permute-start.2) | collective-permute-done | bytes 262176 | tf_op jit(solution)/shard_map/ppermute | solution.py:34
  215.2 13.0 %collective-permute-start.1 = (bf16[8,128,128]{2,1,0:T(8,128)(2,1)}, bf16[8,128,128]{2,1,0:T(8,128)(2,1)}, u32[]{:S(2)}, u32[]{:S(2)}) collective-permute-start(bf16[8,128,128]{2,1,0:T(8,128)(2,1)} %convert_bitcast_fusion.2), channel_id=1, source_target_pairs={{0,1},{1,2},{2,3},{4,5},{5,6},{6,7},{8,9},{9,10},{10,11},{12,13},{... | collective-permute-start | bytes 786440 | tf_op jit(solution)/shard_map/ppermute | solution.py:34
  231.5 7.3 collective-permute-done.1
  241.3 3.6 multiply_reduce_fusion.6
  246.9 6.8 fusion.6
  253.7 5.0 multiply_convert_fusion.1
  258.8 3.5 convolution_convert_fusion.1
  262.3 7.5 multiply_reduce_fusion.4
  271.4 24.4 %pad_maximum_fusion = bf16[8448,1024]{1,0:T(8,128)(2,1)} fusion(bf16[2816,1024]{1,0:T(8,128)(2,1)S(1)} %fusion.122, bf16[5632,1024]{1,0:T(8,128)(2,1)S(1)} %convolution_convert_fusion.1), kind=kLoop, calls=%fused_computation | loop fusion | flops 34603008 | bytes 34603008 | tf_op jit(solution)/shard_map/concatenate | solution.py:306
  296.9 3.8 fusion.20.mix_ref
  300.7 2.5 shard_map.229
  313.0 45.1 %collective-permute-done.8 = bf16[8,128,128]{2,1,0:T(8,128)(2,1)S(1)} collective-permute-done((bf16[8,128,128]{2,1,0:T(8,128)(2,1)}, bf16[8,128,128]{2,1,0:T(8,128)(2,1)S(1)}, u32[]{:S(2)}, u32[]{:S(2)}) %collective-permute-start.8) | collective-permute-done | bytes 262176 | tf_op jit(solution)/shard_map/ppermute | solution.py:34
  362.0 6.1 collective-permute-done.7
  371.5 7.9 shard_map.230
  396.1 3.4 collective-permute-done.13
  399.7 2.8 fusion.54
  404.4 3.2 convolution_convert_fusion.3
  407.6 4.9 convolution_convert_fusion
  412.6 10.4 pad_maximum_fusion.1
  424.3 4.5 fusion.38
  429.8 93.2 %all-reduce.12.cloned.1.call-done = f32[35088]{0:T(1024)} async-done(((f32[35088]{0:T(1024)}), f32[35088]{0:T(1024)}) %all-reduce.12.cloned.1.call-update) | async-done | bytes 140368 | tf_op jit(solution)/shard_map/psum | solution.py:582
  524.7 202.1 %reduce-scatter.5.cloned.1.call-done = bf16[264,1024]{1,0:T(8,128)(2,1)} async-done(((bf16[8448,1024]{1,0:T(8,128)(2,1)}), bf16[264,1024]{1,0:T(8,128)(2,1)}) %reduce-scatter.5.cloned.1.call-update) | async-done | bytes 540688 | tf_op jit(solution)/shard_map/reduce_scatter | solution.py:312
  726.8 3.8 multiply_subtract_fusion
  730.6 355.4 %reduce-scatter.3.cloned.1.call-done = bf16[256,1024]{1,0:T(8,128)(2,1)} async-done(((bf16[8192,1024]{1,0:T(8,128)(2,1)}), bf16[256,1024]{1,0:T(8,128)(2,1)}) %reduce-scatter.3.cloned.1.call-update) | async-done | bytes 524304 | tf_op jit(solution)/shard_map/reduce_scatter | solution.py:312
  1086.0 4.0 multiply_subtract_fusion.1
  (282 shorter events, 76.5 us)
Async XLA Ops:
  7.2 121.4 %copy-start.23 = (f32[1,128,1024]{2,1,0:T(8,128)S(1)}, f32[1,128,1024]{2,1,0:T(8,128)}, u32[]{:S(2)}) copy-start(f32[1,128,1024]{2,1,0:T(8,128)} %param.12) | copy-start | bytes 1572868
  7.2 121.3 %all-gather.3.cloned.1.call-start = ((), (), s32[]{:S(2)}) async-start(), calls=%async_computation.2 | async-start | bytes 17301504 | tf_op jit(solution)/shard_map/all_gather | solution.py:335
  9.5 124.8 %copy-start.75 = (s32[1,512]{1,0:T(1,128)S(1)}, s32[1,512]{1,0:T(1,128)}, u32[]{:S(2)}) copy-start(s32[1,512]{1,0:T(1,128)} %param.13) | copy-start | bytes 6148
  9.5 237.4 %all-gather.5.cloned.1.call-start = ((), (), s32[]{:S(2)}) async-start(), calls=%async_computation.3 | async-start | bytes 17842176 | tf_op jit(solution)/shard_map/all_gather | solution.py:341
  128.6 394.4 %all-reduce.12.cloned.1.call-start = ((), (), s32[]{:S(2)}) async-start(), calls=%async_computation.6 | async-start | bytes 286720 | tf_op jit(solution)/shard_map/psum | solution.py:582
  130.1 22.6 %collective-permute-start = (bf16[3,1024]{1,0:T(4,128)(2,1)S(1)}, bf16[3,1024]{1,0:T(4,128)(2,1)S(1)}, u32[]{:S(2)}, u32[]{:S(2)}) collective-permute-start(bf16[3,1024]{1,0:T(4,128)(2,1)S(1)} %slice.178), channel_id=1, source_target_pairs={{0,1},{1,2},{2,3},{4,5},{5,6},{6,7},{8,9},{9,10},{10,11},{12,13},{... | collective-permute-start | bytes 18440 | tf_op jit(solution)/shard_map/ppermute | solution.py:34
  172.7 55.5 %collective-permute-start.5 = (bf16[8,128,256]{2,1,0:T(8,128)(2,1)}, bf16[8,128,256]{2,1,0:T(8,128)(2,1)S(1)}, u32[]{:S(2)}, u32[]{:S(2)}) collective-permute-start(bf16[8,128,256]{2,1,0:T(8,128)(2,1)} %convert_bitcast_fusion.1), channel_id=1, source_target_pairs={{0,2},{1,3},{4,6},{5,7},{8,10},{9,11},{12,14},{13,15},{16,18},{17,... | collective-permute-start | bytes 1572872 | tf_op jit(solution)/shard_map/ppermute | solution.py:34
  175.4 54.3 %collective-permute-start.4 = (bf16[8,128,256]{2,1,0:T(8,128)(2,1)}, bf16[8,128,256]{2,1,0:T(8,128)(2,1)}, u32[]{:S(2)}, u32[]{:S(2)}) collective-permute-start(bf16[8,128,256]{2,1,0:T(8,128)(2,1)} %convert_bitcast_fusion.1), channel_id=1, source_target_pairs={{0,3},{4,7},{8,11},{12,15},{16,19},{20,23},{24,27},{28,31}} | collective-permute-start | bytes 1572872 | tf_op jit(solution)/shard_map/ppermute | solution.py:34
  178.2 36.9 %collective-permute-start.2 = (bf16[8,128,128]{2,1,0:T(8,128)(2,1)}, bf16[8,128,128]{2,1,0:T(8,128)(2,1)S(1)}, u32[]{:S(2)}, u32[]{:S(2)}) collective-permute-start(bf16[8,128,128]{2,1,0:T(8,128)(2,1)} %convert_bitcast_fusion.2), channel_id=1, source_target_pairs={{0,2},{1,3},{4,6},{5,7},{8,10},{9,11},{12,14},{13,15},{16,18},{17,... | collective-permute-start | bytes 786440 | tf_op jit(solution)/shard_map/ppermute | solution.py:34
  179.5 48.6 %collective-permute-start.3 = (bf16[8,128,128]{2,1,0:T(8,128)(2,1)}, bf16[8,128,128]{2,1,0:T(8,128)(2,1)S(1)}, u32[]{:S(2)}, u32[]{:S(2)}) collective-permute-start(bf16[8,128,128]{2,1,0:T(8,128)(2,1)} %convert_bitcast_fusion.2), channel_id=1, source_target_pairs={{0,3},{4,7},{8,11},{12,15},{16,19},{20,23},{24,27},{28,31}} | collective-permute-start | bytes 786440 | tf_op jit(solution)/shard_map/ppermute | solution.py:34
  180.8 57.9 %collective-permute-start.6 = (bf16[8,128,256]{2,1,0:T(8,128)(2,1)}, bf16[8,128,256]{2,1,0:T(8,128)(2,1)}, u32[]{:S(2)}, u32[]{:S(2)}) collective-permute-start(bf16[8,128,256]{2,1,0:T(8,128)(2,1)} %convert_bitcast_fusion.1), channel_id=1, source_target_pairs={{0,1},{1,2},{2,3},{4,5},{5,6},{6,7},{8,9},{9,10},{10,11},{12,13},{... | collective-permute-start | bytes 1572872 | tf_op jit(solution)/shard_map/ppermute | solution.py:34
  183.8 56.5 %copy-start.1 = (f32[128,2048]{1,0:T(8,128)}, f32[128,2048]{1,0:T(8,128)S(1)}, u32[]{:S(2)}) copy-start(f32[128,2048]{1,0:T(8,128)S(1)} %slice.186.gate_ref) | copy-start | bytes 3145732
  215.2 23.6 %collective-permute-start.1 = (bf16[8,128,128]{2,1,0:T(8,128)(2,1)}, bf16[8,128,128]{2,1,0:T(8,128)(2,1)}, u32[]{:S(2)}, u32[]{:S(2)}) collective-permute-start(bf16[8,128,128]{2,1,0:T(8,128)(2,1)} %convert_bitcast_fusion.2), channel_id=1, source_target_pairs={{0,1},{1,2},{2,3},{4,5},{5,6},{6,7},{8,9},{9,10},{10,11},{12,13},{... | collective-permute-start | bytes 786440 | tf_op jit(solution)/shard_map/ppermute | solution.py:34
  244.9 51.0 %copy-start.29 = (f32[128,1024]{1,0:T(8,128)}, f32[128,1024]{1,0:T(8,128)S(1)}, u32[]{:S(2)}) copy-start(f32[128,1024]{1,0:T(8,128)S(1)} %get-tuple-element.121) | copy-start | bytes 1572868
  305.1 54.4 %collective-permute-start.11 = (bf16[8,128,256]{2,1,0:T(8,128)(2,1)}, bf16[8,128,256]{2,1,0:T(8,128)(2,1)S(1)}, u32[]{:S(2)}, u32[]{:S(2)}) collective-permute-start(bf16[8,128,256]{2,1,0:T(8,128)(2,1)} %convert_bitcast_fusion), channel_id=1, source_target_pairs={{2,0},{3,1},{6,4},{7,5},{10,8},{11,9},{14,12},{15,13},{18,16},{19,... | collective-permute-start | bytes 1572872 | tf_op jit(solution)/shard_map/ppermute | solution.py:34
  306.4 53.9 %collective-permute-start.10 = (bf16[8,128,256]{2,1,0:T(8,128)(2,1)}, bf16[8,128,256]{2,1,0:T(8,128)(2,1)}, u32[]{:S(2)}, u32[]{:S(2)}) collective-permute-start(bf16[8,128,256]{2,1,0:T(8,128)(2,1)} %convert_bitcast_fusion), channel_id=1, source_target_pairs={{3,0},{7,4},{11,8},{15,12},{19,16},{23,20},{27,24},{31,28}} | collective-permute-start | bytes 1572872 | tf_op jit(solution)/shard_map/ppermute | solution.py:34
  307.7 50.5 %collective-permute-start.8 = (bf16[8,128,128]{2,1,0:T(8,128)(2,1)}, bf16[8,128,128]{2,1,0:T(8,128)(2,1)S(1)}, u32[]{:S(2)}, u32[]{:S(2)}) collective-permute-start(bf16[8,128,128]{2,1,0:T(8,128)(2,1)} %convert_bitcast_fusion.2), channel_id=1, source_target_pairs={{2,0},{3,1},{6,4},{7,5},{10,8},{11,9},{14,12},{15,13},{18,16},{19,... | collective-permute-start | bytes 786440 | tf_op jit(solution)/shard_map/ppermute | solution.py:34
  309.0 50.5 %collective-permute-start.9 = (bf16[8,128,128]{2,1,0:T(8,128)(2,1)}, bf16[8,128,128]{2,1,0:T(8,128)(2,1)}, u32[]{:S(2)}, u32[]{:S(2)}) collective-permute-start(bf16[8,128,128]{2,1,0:T(8,128)(2,1)} %convert_bitcast_fusion.2), channel_id=1, source_target_pairs={{3,0},{7,4},{11,8},{15,12},{19,16},{23,20},{27,24},{31,28}} | collective-permute-start | bytes 786440 | tf_op jit(solution)/shard_map/ppermute | solution.py:34
  310.3 57.9 %collective-permute-start.12 = (bf16[8,128,256]{2,1,0:T(8,128)(2,1)}, bf16[8,128,256]{2,1,0:T(8,128)(2,1)}, u32[]{:S(2)}, u32[]{:S(2)}) collective-permute-start(bf16[8,128,256]{2,1,0:T(8,128)(2,1)} %convert_bitcast_fusion), channel_id=1, source_target_pairs={{1,0},{2,1},{3,2},{5,4},{6,5},{7,6},{9,8},{10,9},{11,10},{13,12},{... | collective-permute-start | bytes 1572872 | tf_op jit(solution)/shard_map/ppermute | solution.py:34
  313.0 57.5 %copy-start.5 = (f32[128,2048]{1,0:T(8,128)S(1)}, f32[128,2048]{1,0:T(8,128)}, u32[]{:S(2)}) copy-start(f32[128,2048]{1,0:T(8,128)} %copy-done.4) | copy-start | bytes 3145732
  313.0 57.5 %copy-start.12 = (f32[1,8,128,128]{3,2,1,0:T(8,128)S(1)}, f32[1,8,128,128]{3,2,1,0:T(8,128)}, u32[]{:S(2)}) copy-start(f32[1,8,128,128]{3,2,1,0:T(8,128)} %copy-done.11) | copy-start | bytes 1572868
  358.1 10.0 collective-permute-start.7
  393.6 5.9 collective-permute-start.13
  403.3 323.5 %reduce-scatter.5.cloned.1.call-start = ((), (), s32[]{:S(2)}) async-start(), calls=%async_computation.5 | async-start | bytes 17842176 | tf_op jit(solution)/shard_map/reduce_scatter | solution.py:312
  403.9 682.1 %reduce-scatter.3.cloned.1.call-start = ((), (), s32[]{:S(2)}) async-start(), calls=%async_computation.4 | async-start | bytes 17301504 | tf_op jit(solution)/shard_map/reduce_scatter | solution.py:312
  424.2 98.7 %copy-start.44 = (f32[35088]{0:T(1024)S(1)}, f32[35088]{0:T(1024)}, u32[]{:S(2)}) copy-start(f32[35088]{0:T(1024)} %param.21) | copy-start | bytes 421060
  424.2 98.7 %copy-start.53 = (f32[35088]{0:T(1024)S(1)}, f32[35088]{0:T(1024)}, u32[]{:S(2)}) copy-start(f32[35088]{0:T(1024)} %param.22) | copy-start | bytes 421060
  424.2 98.7 %copy-start.54 = (f32[35088]{0:T(1024)S(1)}, f32[35088]{0:T(1024)}, u32[]{:S(2)}) copy-start(f32[35088]{0:T(1024)} %param.23) | copy-start | bytes 421060
  428.7 298.0 %copy-start.26 = (f32[264,1024]{1,0:T(8,128)S(1)}, f32[264,1024]{1,0:T(8,128)}, u32[]{:S(2)}) copy-start(f32[264,1024]{1,0:T(8,128)} %param.18) | copy-start | bytes 3244036
  428.8 298.0 %copy-start.35 = (f32[264,1024]{1,0:T(8,128)S(1)}, f32[264,1024]{1,0:T(8,128)}, u32[]{:S(2)}) copy-start(f32[264,1024]{1,0:T(8,128)} %param.19) | copy-start | bytes 3244036
  524.7 561.3 %copy-start.27 = (f32[256,1024]{1,0:T(8,128)S(1)}, f32[256,1024]{1,0:T(8,128)}, u32[]{:S(2)}) copy-start(f32[256,1024]{1,0:T(8,128)} %param.15) | copy-start | bytes 3145732
  730.6 359.5 %copy-start.38 = (f32[35088]{0:T(1024)S(1)}, f32[35088]{0:T(1024)}, u32[]{:S(2)}) copy-start(f32[35088]{0:T(1024)} %all-reduce.12.cloned.1.call-done) | copy-start | bytes 421060
  (75 other events, 431.2 us)
Sparse Core Ops, SparseCore 0:
  11.5 117.0 all-gather.2
  132.0 114.8 all-gather.4
  403.4 119.5 all-reduce.11
  529.2 197.4 reduce-scatter.4
  728.9 357.0 reduce-scatter.2
where the time goes:
time: 1110 us; the launch traced here: 1100 us
  waiting for transfers between devices  865 us (78%)
  matrix products  70.2 us (6%)
  other arithmetic  66.7 us (6%)
  starting transfers between devices  35 us (3%)
  local copies, waits for them, and re-layouts  24.4 us (2%)
  Pallas kernels  21.2 us (2%)
  between operations  15.3 us (1%)
    reduce_scatter x2, waiting for transfers between devices, to_owners(): lax.psum_scatter(rows, ('dp', 'ctx'), scatter_dimension=0, tiled=True)  558 us
    all_gather x1, waiting for transfers between devices, per_device(): lax.all_gather(mixer_params.astype(jnp.bfloat16), ('dp', 'ctx'), axis=0,...  118 us
    ppermute x14, waiting for transfers between devices, passed_along(): return lax.ppermute(shard, axis, pairs)  93.4 us
    psum x1, waiting for transfers between devices, per_device(): small_grad = lax.psum(small_local, ('dp', 'ctx'))  93.2 us
    concatenate x2, other arithmetic, owner_rows(): jnp.concatenate([product(first_left, first_right), product(second_left, s...  34.8 us
    ppermute x14, starting transfers between devices, passed_along(): return lax.ppermute(shard, axis, pairs)  34.8 us
  transfers between devices with their start and end apart: 19, of which 10 were waited for; matrix products, arithmetic and copies ran while one was open for 7% of the time, Pallas kernels for 1%

commit v1 on v0

--- a/solution.py
+++ b/solution.py
@@ -1,3 +1,6 @@
+import functools
+import heapq
+
 import jax
 import jax.numpy as jnp
 from jax import lax
@@ -314,6 +317,529 @@
     )
 
 
+def ranks_of(extent):
+    return [0] + [side * step for step in range(1, extent) for side in (1, -1)]
+
+
+def route_slots(order, extents):
+    found = [{}]
+    for dim in order:
+        values = ranks_of(extents[dim]) if dim == "z" else list(range(extents[dim]))
+        found = [dict(one, **{dim: value}) for one in found for value in values]
+    return found
+
+
+def slot_key(slot):
+    return (slot["z"], slot["y"], slot["x"])
+
+
+def route_children(slot, order, extents):
+    reached = max([i for i, dim in enumerate(order) if slot[dim] != 0], default=-1)
+    found = []
+    for i, dim in enumerate(order):
+        if i < reached:
+            continue
+        if dim == "z":
+            sides = (1, -1) if i > reached else ((-1,) if slot["z"] > 0 else (1,))
+            for side in sides:
+                child = dict(slot, z=slot["z"] - side)
+                if abs(child["z"]) < extents["z"]:
+                    found.append((dim, side, child))
+        elif i > reached:
+            found.append((dim, 0, dict(slot, **{dim: 1})))
+    return found
+
+
+def route_order(parts, extents):
+    chips = [
+        (z, y, x) for z in range(extents["z"]) for y in range(extents["y"]) for x in range(extents["x"])
+    ]
+    free, events, seen = ({}, [], {})
+    for chip in chips:
+        for part in range(len(parts)):
+            events.append((0.0, chip, part, (0, 0, 0)))
+    heapq.heapify(events)
+    while events:
+        now, chip, part, key = heapq.heappop(events)
+        seen.setdefault((part, key), []).append(now)
+        slot = dict(zip(("z", "y", "x"), key))
+        for dim, side, child in route_children(slot, parts[part][2], extents):
+            if dim == "z":
+                there = (chip[0] + side, chip[1], chip[2])
+                if not 0 <= there[0] < extents["z"]:
+                    continue
+            elif dim == "y":
+                there = (chip[0], 1 - chip[1], chip[2])
+            else:
+                there = (chip[0], chip[1], 1 - chip[2])
+            end = max(now, free.get((chip, there), 0.0)) + parts[part][1]
+            free[chip, there] = end
+            heapq.heappush(events, (end + 22.0, there, part, slot_key(child)))
+    return sorted(seen, key=lambda one: (sum(seen[one]) / len(seen[one]), one))
+
+
+def row_parts(rows):
+    first = (rows * 3 // 8) // 16 * 16
+    second = (rows * 7 // 16) // 16 * 16
+    return [
+        (0, first, ("z", "x", "y")),
+        (first, second, ("z", "y", "x")),
+        (first + second, rows - first - second, ("x", "y", "z")),
+    ]
+
+
+class Place:
+    def __init__(self, extents):
+        dp, ctx = (lax.axis_index("dp"), lax.axis_index("ctx"))
+        self.extents = extents
+        self.z, self.core = (dp // 2, dp % 2)
+        self.y, self.x = (ctx // 2, ctx % 2)
+        self.dp, self.ctx = (dp, ctx)
+
+    def valid(self, slot):
+        if slot["z"] == 0:
+            return None
+        z = self.z + slot["z"]
+        return (z >= 0) & (z < self.extents["z"])
+
+    def source(self, slot):
+        y = self.y if slot["y"] == 0 else 1 - self.y
+        x = self.x if slot["x"] == 0 else 1 - self.x
+        return (self.z + slot["z"], y, x)
+
+    def chip_index(self, slot):
+        z, y, x = self.source(slot)
+        return (z * 2 + y) * 2 + x
+
+    def shard_index(self, slot, core):
+        z, y, x = self.source(slot)
+        return ((z * 2 + core) * 2 + y) * 2 + x
+
+    def neighbour(self, dim, side):
+        if dim == "z":
+            return (self.dp + 2 * side, self.ctx)
+        if dim == "core":
+            return (self.dp + 1 - 2 * self.core, self.ctx)
+        if dim == "y":
+            return (self.dp, (1 - self.y) * 2 + self.x)
+        return (self.dp, self.y * 2 + 1 - self.x)
+
+    def has(self, dim, side):
+        if dim != "z":
+            return None
+        return (self.z + side < self.extents["z"]) if side > 0 else (self.z + side >= 0)
+
+    def greet(self, whole=False):
+        barrier = pltpu.get_barrier_semaphore()
+        total = 3
+        for dim in ("core", "x", "y"):
+            pl.semaphore_signal(barrier, 1, device_id=self.neighbour(dim, 0), device_id_type=MESH)
+        if whole:
+            for z in range(self.extents["z"]):
+
+                @pl.when(self.z != z)
+                def _():
+                    pl.semaphore_signal(
+                        barrier, 1, device_id=(2 * z + self.core, self.ctx), device_id_type=MESH
+                    )
+
+            total = total + self.extents["z"] - 1
+        else:
+            for side in (1, -1):
+                near = self.has("z", side)
+
+                @pl.when(near)
+                def _():
+                    pl.semaphore_signal(
+                        barrier, 1, device_id=self.neighbour("z", side), device_id_type=MESH
+                    )
+
+                total = total + near.astype(jnp.int32)
+        pl.semaphore_wait(barrier, total)
+
+
+MESH = pl.DeviceIdType.MESH
+
+
+def both(left, right):
+    if left is None:
+        return right
+    return left if right is None else left & right
+
+
+def guarded(condition, body):
+    if condition is None:
+        body()
+    else:
+        pl.when(condition)(body)
+
+
+def drain(ref, sem):
+    pltpu.make_async_copy(ref, ref, sem).wait()
+
+
+def gather_kernel(
+    extents, parts, order, shard_ref, out_ref, got, side_got, side_sent, flat_sent, z_sent, own_sem
+):
+    place = Place(extents)
+    chips = extents["z"] * extents["y"] * extents["x"]
+    rank = {}
+    for part, (_, _, dims) in enumerate(parts):
+        for slot in route_slots(dims, extents):
+            rank[part, slot_key(slot)] = len(rank)
+    place.greet()
+    mine = place.shard_index({"z": 0, "y": 0, "x": 0}, place.core)
+    own = pltpu.make_async_copy(shard_ref, out_ref.at[mine], own_sem)
+    own.start()
+    waits = []
+    for part, key in order:
+        start, rows, dims = parts[part]
+        slot = dict(zip(("z", "y", "x"), key))
+        number = rank[part, key]
+
+        def step(part=part, key=key, start=start, rows=rows, dims=dims, slot=slot, number=number):
+            block = out_ref.at[place.shard_index(slot, place.core), pl.ds(start, rows)]
+            held = shard_ref.at[pl.ds(start, rows)] if key == (0, 0, 0) else block
+            if key != (0, 0, 0):
+                drain(block, got.at[number])
+            for dim, side, child in route_children(slot, dims, extents):
+                there = rank[part, slot_key(child)]
+                if dim == "z":
+                    sent = z_sent.at[number, (side + 1) // 2]
+                else:
+                    sent = flat_sent.at[part, 0 if dim == "x" else 1]
+                copy = pltpu.make_async_remote_copy(
+                    src_ref=held,
+                    dst_ref=block,
+                    send_sem=sent,
+                    recv_sem=got.at[there],
+                    device_id=place.neighbour(dim, side),
+                    device_id_type=MESH,
+                )
+                guarded(place.has(dim, side), copy.start)
+            pltpu.make_async_remote_copy(
+                src_ref=held,
+                dst_ref=block,
+                send_sem=side_sent,
+                recv_sem=side_got,
+                device_id=place.neighbour("core", 0),
+                device_id_type=MESH,
+            ).start()
+
+        guarded(place.valid(slot), step)
+        for dim, side, _ in route_children(slot, dims, extents):
+            if dim == "z":
+                waits.append((slot, side, start, rows, z_sent.at[number, (side + 1) // 2]))
+    own.wait()
+    drain(out_ref.at[pl.ds(0, chips)], side_got)
+    drain(out_ref.at[pl.ds(0, chips)], side_sent)
+    for part, (start, rows, dims) in enumerate(parts):
+        counts = {"x": 0, "y": 0}
+        for slot in route_slots(dims, extents):
+            if slot["z"] < 0:
+                continue
+            for dim, _, _ in route_children(slot, dims, extents):
+                if dim != "z":
+                    counts[dim] = counts[dim] + 1
+        for dim in ("x", "y"):
+            drain(
+                out_ref.at[pl.ds(0, counts[dim]), pl.ds(start, rows)],
+                flat_sent.at[part, 0 if dim == "x" else 1],
+            )
+    for slot, side, start, rows, sent in waits:
+        guarded(
+            both(place.valid(slot), place.has("z", side)),
+            functools.partial(drain, out_ref.at[0, pl.ds(start, rows)], sent),
+        )
+
+
+def gathered(shard, extents, number):
+    rows, columns = shard.shape
+    total = 2 * extents["z"] * extents["y"] * extents["x"]
+    parts = row_parts(rows)
+    order = route_order(parts, extents)
+    slots = len(order)
+    whole = pl.pallas_call(
+        functools.partial(gather_kernel, extents, parts, order),
+        out_shape=jax.ShapeDtypeStruct((total, rows, columns), shard.dtype),
+        in_specs=[pl.BlockSpec(memory_space=pltpu.VMEM)],
+        out_specs=pl.BlockSpec(memory_space=pl.ANY),
+        scratch_shapes=[
+            pltpu.SemaphoreType.DMA((slots,)),
+            pltpu.SemaphoreType.DMA,
+            pltpu.SemaphoreType.DMA,
+            pltpu.SemaphoreType.DMA((len(parts), 2)),
+            pltpu.SemaphoreType.DMA((slots, 2)),
+            pltpu.SemaphoreType.DMA,
+        ],
+        compiler_params=pltpu.CompilerParams(collective_id=number, has_side_effects=True),
+    )(shard)
+    return whole.reshape(total * rows, columns)
+
+
+CHILD_SEM = {("z", 1): 0, ("z", -1): 1, ("x", 0): 2, ("y", 0): 3}
+
+
+def route_parent(slot):
+    def up(dims):
+        last = max(i for i, dim in enumerate(dims) if slot[dim] != 0)
+        dim = dims[last]
+        if dim != "z":
+            return (dim, 0, 0, dict(slot, **{dim: 0}))
+        side = 1 if slot["z"] > 0 else -1
+        return (dim, side, -side, dict(slot, z=slot["z"] - side))
+
+    return up
+
+
+def child_rooms(dims, extents):
+    rooms, base = ({}, 0)
+    for i, dim in enumerate(dims):
+        names = dims[:i] + (("z",) if dim == "z" else ())
+        size = 1
+        for name in names:
+            size = size * extents[name]
+        for side in (1, -1) if dim == "z" else (0,):
+            rooms[dim, side] = (base, names)
+            base = base + size
+    return (rooms, base)
+
+
+def small_steps(place, small_ref, total_ref, room_ref, small_got, small_sent):
+    axes = ["core", "x", "y", "z"]
+    spot = {"core": place.core, "x": place.x, "y": place.y, "z": place.z}
+    count = dict(place.extents, core=2)
+
+    def peer(dim, other):
+        if dim == "z":
+            return (other * 2 + place.core, place.ctx)
+        return place.neighbour(dim, 0)
+
+    def send(level):
+        dim = axes[level]
+        mine = spot[dim]
+        source = small_ref if level == 0 else total_ref.at[level - 1]
+        room_ref[level, mine] = source[...]
+        for other in range(count[dim]):
+            copy = pltpu.make_async_remote_copy(
+                src_ref=source,
+                dst_ref=room_ref.at[level, mine],
+                send_sem=small_sent.at[level, other],
+                recv_sem=small_got.at[level, mine],
+                device_id=peer(dim, other),
+                device_id_type=MESH,
+            )
+            pl.when(mine != other)(copy.start)
+
+    def finish(level):
+        dim = axes[level]
+        mine = spot[dim]
+        for other in range(count[dim]):
+            room = room_ref.at[level, other]
+            pl.when(mine != other)(functools.partial(drain, room, small_got.at[level, other]))
+        value = room_ref[level, 0]
+        for other in range(1, count[dim]):
+            value = value + room_ref[level, other]
+        total_ref[level] = value
+        if level + 1 < len(axes):
+            send(level + 1)
+
+    def close():
+        for level, dim in enumerate(axes):
+            for other in range(count[dim]):
+                pl.when(spot[dim] != other)(
+                    functools.partial(drain, room_ref.at[level, 0], small_sent.at[level, other])
+                )
+
+    return (send, finish, close)
+
+
+def scatter_kernel(extents, parts, order, small, *refs):
+    left_ref, right_ref, refs = (refs[0], refs[1], refs[2:])
+    if small:
+        small_ref, out_ref, total_ref, refs = (refs[0], refs[1], refs[2], refs[3:])
+    else:
+        out_ref, refs = (refs[0], refs[1:])
+    count = len(parts)
+    stages, sides, rooms, accs = [refs[i * count : (i + 1) * count] for i in range(4)]
+    side_got, child_got, side_sent, sent = refs[4 * count : 4 * count + 4]
+    place = Place(extents)
+    chips = extents["z"] * extents["y"] * extents["x"]
+    rank = {}
+    for part, (_, _, dims) in enumerate(parts):
+        for slot in route_slots(dims, extents):
+            rank[part, slot_key(slot)] = len(rank)
+    place.greet(whole=small)
+    if small:
+        send, finish, close = small_steps(place, small_ref, total_ref, *refs[4 * count + 4 :])
+        send(0)
+
+    def product(slot, part, core):
+        start, rows, _ = parts[part]
+        return dot(left_ref[place.shard_index(slot, core), pl.ds(start, rows)], right_ref[...])
+
+    def room_index(part, slot, dim, side):
+        z, y, x = place.source(slot)
+        spot = {"z": z, "y": y, "x": x}
+        base, names = child_rooms(parts[part][2], extents)[0][dim, side]
+        index = 0
+        for name in names:
+            index = index * extents[name] + spot[name]
+        return base + index
+
+    def hand_over(part, key):
+        slot = dict(zip(("z", "y", "x"), key))
+
+        def step():
+            chip = place.chip_index(slot)
+            stage = stages[part].at[chip]
+            stage[...] = product(slot, part, 1 - place.core).astype(jnp.bfloat16)
+            pltpu.make_async_remote_copy(
+                src_ref=stage,
+                dst_ref=sides[part].at[chip],
+                send_sem=side_sent.at[part],
+                recv_sem=side_got.at[rank[part, key]],
+                device_id=place.neighbour("core", 0),
+                device_id_type=MESH,
+            ).start()
+
+        guarded(place.valid(slot), step)
+
+    def merge(part, key):
+        start, rows, dims = parts[part]
+        slot = dict(zip(("z", "y", "x"), key))
+        number = rank[part, key]
+
+        def step():
+            side = sides[part].at[place.chip_index(slot)]
+            acc = accs[part]
+            acc[...] = product(slot, part, place.core)
+            drain(side, side_got.at[number])
+            acc[...] += side[...].astype(jnp.float32)
+            for dim, sign, _ in route_children(slot, dims, extents):
+                room = rooms[part].at[room_index(part, slot, dim, sign)]
+                got = child_got.at[number, CHILD_SEM[dim, sign]]
+
+                def take(room=room, got=got):
+                    drain(room, got)
+                    acc[...] += room[...].astype(jnp.float32)
+
+                guarded(place.has(dim, sign), take)
+            if key == (0, 0, 0):
+                out_ref[pl.ds(start, rows)] = acc[...]
+                return
+            side[...] = acc[...].astype(jnp.bfloat16)
+            dim, sign, seen, parent = route_parent(slot)(dims)
+            pltpu.make_async_remote_copy(
+                src_ref=side,
+                dst_ref=rooms[part].at[room_index(part, slot, dim, seen)],
+                send_sem=sent.at[part],
+                recv_sem=child_got.at[rank[part, slot_key(parent)], CHILD_SEM[dim, seen]],
+                device_id=place.neighbour(dim, sign),
+                device_id_type=MESH,
+            ).start()
+
+        guarded(place.valid(slot), step)
+
+    ahead = 8
+    for one in order[:ahead]:
+        hand_over(*one)
+    for i, one in enumerate(order):
+        if i + ahead < len(order):
+            hand_over(*order[i + ahead])
+        merge(*one)
+        if small and (i + 1) % (len(order) // 5) == 0 and (i + 1) // (len(order) // 5) <= 4:
+            finish((i + 1) // (len(order) // 5) - 1)
+    if small:
+        close()
+    for part in range(count):
+        drain(stages[part], side_sent.at[part])
+        drain(sides[part].at[pl.ds(0, chips - 1)], sent.at[part])
+
+
+def scattered(left, right, small, extents, number):
+    total, rows, depth = left.shape
+    columns = right.shape[1]
+    chips = total // 2
+    parts = row_parts(rows)
+    order = list(reversed(route_order(parts, extents)))
+    slots = len(order)
+    vmem = pl.BlockSpec(memory_space=pltpu.VMEM)
+    args = (left, right)
+    outs = [jax.ShapeDtypeStruct((rows, columns), jnp.float32)]
+    scratch = (
+        [pltpu.VMEM((chips, size, columns), jnp.bfloat16) for _, size, _ in parts]
+        + [pltpu.VMEM((chips, size, columns), jnp.bfloat16) for _, size, _ in parts]
+        + [
+            pltpu.VMEM((child_rooms(dims, extents)[1], size, columns), jnp.bfloat16)
+            for _, size, dims in parts
+        ]
+        + [pltpu.VMEM((size, columns), jnp.float32) for _, size, _ in parts]
+        + [
+            pltpu.SemaphoreType.DMA((slots,)),
+            pltpu.SemaphoreType.DMA((slots, 4)),
+            pltpu.SemaphoreType.DMA((len(parts),)),
+            pltpu.SemaphoreType.DMA((len(parts),)),
+        ]
+    )
+    if small is not None:
+        args = args + (small,)
+        outs.append(jax.ShapeDtypeStruct((4,) + small.shape, jnp.float32))
+        most = max(2, extents["z"])
+        scratch = scratch + [
+            pltpu.VMEM((4, most) + small.shape, jnp.float32),
+            pltpu.SemaphoreType.DMA((4, most)),
+            pltpu.SemaphoreType.DMA((4, most)),
+        ]
+    return pl.pallas_call(
+        functools.partial(scatter_kernel, extents, parts, order, small is not None),
+        out_shape=outs,
+        in_specs=[vmem] * len(args),
+        out_specs=[vmem] * len(outs),
+        scratch_shapes=scratch,
+        compiler_params=pltpu.CompilerParams(
+            collective_id=number, has_side_effects=True, vmem_limit_bytes=56 * 1024 * 1024
+        ),
+    )(*args)
+
+
+def routed():
+    return lax.axis_size("ctx") == 4 and lax.axis_size("dp") % 2 == 0
+
+
+def route_extents():
+    return {"z": lax.axis_size("dp") // 2, "y": 2, "x": 2}
+
+
+def all_rows(shard, number):
+    if routed():
+        return gathered(shard, route_extents(), number)
+    return lax.all_gather(shard, ("dp", "ctx"), axis=0, tiled=True)
+
+
+def owner_sums(first_left, first_right, second_left, second_right, small, number):
+    if not routed():
+        grad = to_owners(owner_rows(first_left, first_right, second_left, second_right))
+        return (grad, None if small is None else lax.psum(small, ("dp", "ctx")))
+    tokens = first_left.shape[0]
+    left = jnp.concatenate(
+        [
+            jnp.pad(first_left.T, ((0, 0), (0, tokens))),
+            jnp.pad(second_left.T, ((0, 0), (tokens, 0))),
+        ]
+    )
+    devices = lax.axis_size("dp") * lax.axis_size("ctx")
+    left = left.reshape(devices, left.shape[0] // devices, 2 * tokens)
+    right = jnp.concatenate([first_right, second_right])
+    if small is None:
+        return (scattered(left, right, None, route_extents(), number)[0], None)
+    extent = small.shape[0]
+    rows = -(-extent // 1024) * 8
+    packed = jnp.pad(small, (0, rows * 128 - extent)).reshape(rows, 128)
+    grad, totals = scattered(left, right, packed, route_extents(), number)
+    return (grad, totals[3].reshape(-1)[:extent])
+
+
 def shifted(shard, by):
     return passed_along(shard, "ctx", by)
 
@@ -332,13 +858,11 @@
     small_first,
     small_second,
 ):
-    mixer_weights = lax.all_gather(
-        mixer_params.astype(jnp.bfloat16), ("dp", "ctx"), axis=0, tiled=True
-    )
+    mixer_weights = all_rows(mixer_params.astype(jnp.bfloat16), 0)
     feed_half, mixer_weights = lax.optimization_barrier(
         (feed_params.astype(jnp.bfloat16), mixer_weights)
     )
-    feed_weights = lax.all_gather(feed_half, ("dp", "ctx"), axis=0, tiled=True)
+    feed_weights = all_rows(feed_half, 1)
     conv_weight, gain_first, gain_second, out_gain, gate_rows, decay_log, decay_bias = unpack_small(
         small_params
     )
@@ -488,9 +1012,7 @@
     )
     grad_gain_second = jnp.sum(grad_hidden_normed * hidden * inverse_second, axis=0)
     grad_hidden_half = grad_hidden.astype(jnp.bfloat16)
-    feed_rows = owner_rows(grad_gate_up, hidden_normed, middle, cotangent_half)
-    feed_rows, grad_hidden_half = lax.optimization_barrier((feed_rows, grad_hidden_half))
-    feed_grad = to_owners(feed_rows)
+    feed_grad, _ = owner_sums(grad_gate_up, hidden_normed, middle, cotangent_half, None, 2)
     grad_mix = jnp.einsum(
         "td,rd->tr", grad_hidden_half, out_weight, preferred_element_type=jnp.float32
     )
@@ -579,8 +1101,9 @@
             grad_decay_bias,
         ]
     )
-    small_grad = lax.psum(small_local, ("dp", "ctx"))
-    mixer_grad = to_owners(owner_rows(grad_projected, normed, mix_half, grad_hidden_half))
+    mixer_grad, small_grad = owner_sums(
+        grad_projected, normed, mix_half, grad_hidden_half, small_local, 3
+    )
     mixer_new, mixer_moment, mixer_square = adamw(
         mixer_params, mixer_grad, mixer_first, mixer_second
     )

time: 1110 us -> 550 us (0.50)
  waiting for transfers between devices: 865 us -> 9.68 us
  Pallas kernels: 21.2 us -> 352 us
  local copies, waits for them, and re-layouts: 24.4 us -> 42.7 us
  other arithmetic: 66.7 us -> 49.2 us
  matrix products: 70.2 us -> 56.7 us
  between operations: 15.3 us -> 1.99 us
    reduce_scatter x2 -> x0, waiting for transfers between devices: 558 us -> none  [to_owners(): lax.psum_scatter(rows, ('dp', 'ctx'), scatter_dimension=0, tiled=True)]
    pallas_call x0 -> x4, Pallas kernels: none -> 330 us  [the longest x2 178 us: scattered(): pl.pallas_call(functools.partial(scatter_kernel, extents, parts, order, s...]
    all_gather x2 -> x0, waiting for transfers between devices: 120 us -> none  [the longest x1 118 us: per_device(): lax.all_gather(mixer_params.astype(jnp.bfloat16), ('dp', 'ctx'), axis=0,...]
    psum x1 -> x0, waiting for transfers between devices: 93.2 us -> none  [per_device(): small_grad = lax.psum(small_local, ('dp', 'ctx'))]
    ppermute x14, waiting for transfers between devices: 93.4 us -> 9.68 us  [passed_along(): return lax.ppermute(shard, axis, pairs)]
    concatenate x2 -> x4, other arithmetic: 34.8 us -> 16.9 us  [the longest x2 15.2 us: owner_sums(): jnp.concatenate([jnp.pad(first_left.T, ((0, 0), (0, tokens))), jnp.pad(se...]
    dot_general x4 -> x0, matrix products: 13.4 us -> none  [product(): jnp.einsum('tr,td->rd', left_part, right_part, preferred_element_type=jnp...]
    concatenate x0 -> x2, local copies, waits for them, and re-layouts: none -> 12.8 us  [owner_sums(): jnp.concatenate([jnp.pad(first_left.T, ((0, 0), (0, tokens))), jnp.pad(se...]
  transfers between devices with their start and end apart: 19 -> 14, of which waited for: 10 -> 2; matrix products, arithmetic and copies ran while one was open for 7% -> 17% of each run, Pallas kernels for 1% -> 45%
where the time goes in v1:
time: 550 us; the launch traced here: 543 us
  Pallas kernels  352 us (64%)
  matrix products  56.7 us (10%)
  other arithmetic  49.2 us (9%)
  local copies, waits for them, and re-layouts  42.7 us (8%)
  starting transfers between devices  31 us (6%)
  waiting for transfers between devices  9.68 us (2%)
    pallas_call x2, Pallas kernels, scattered(): pl.pallas_call(functools.partial(scatter_kernel, extents, parts, order, s...  178 us
    pallas_call x2, Pallas kernels, gathered(): pl.pallas_call(functools.partial(gather_kernel, extents, parts, order), o...  153 us
    ppermute x14, starting transfers between devices, passed_along(): return lax.ppermute(shard, axis, pairs)  31 us
    pallas_call x4, Pallas kernels, kernel_call(): pl.pallas_call(body, grid=grid, in_specs=in_specs, out_specs=out_specs, o...  21.5 us
    concatenate x2, other arithmetic, owner_sums(): jnp.concatenate([jnp.pad(first_left.T, ((0, 0), (0, tokens))), jnp.pad(se...  15.2 us
    concatenate x2, local copies, waits for them, and re-layouts, owner_sums(): jnp.concatenate([jnp.pad(first_left.T, ((0, 0), (0, tokens))), jnp.pad(se...  12.8 us
  transfers between devices with their start and end apart: 14, of which 2 were waited for; matrix products, arithmetic and copies ran while one was open for 17% of the time, Pallas kernels for 45%

profile of v1, /device:TPU:0, one launch (start us, length us, event | category | flops | bytes accessed | tf_op | source)
XLA Modules:
  0.0 543.3 jit_solution(42338394890521546)
XLA Ops:
  5.0 5.5 %collective-permute-start = (bf16[3,1024]{1,0:T(4,128)(2,1)}, bf16[3,1024]{1,0:T(4,128)(2,1)}, u32[]{:S(2)}, u32[]{:S(2)}) collective-permute-start(bf16[3,1024]{1,0:T(4,128)(2,1)} %slice.186), channel_id=1, source_target_pairs={{0,1},{1,2},{2,3},{4,5},{5,6},{6,7},{8,9},{9,10},{10,11},{12,13},{... | collective-permute-start | bytes 18440 | tf_op jit(solution)/shard_map/ppermute | solution.py:37
  16.6 69.4 %shard_map.227 = bf16[32,256,1024]{2,1,0:T(8,128)(2,1)} custom-call(bf16[256,1024]{1,0:T(8,128)(2,1)} %convert_element_type.111.shard_ref), custom_call_target="tpu_custom_call" | custom-call | tf_op jit(solution)/shard_map/pallas_call | solution.py:562
  86.1 10.5 %fusion.2 = f32[128,6144]{1,0:T(8,128)} fusion(bf16[128,1024]{1,0:T(8,128)(2,1)S(1)} %fusion.55, bf16[8192,1024]{1,0:T(8,128)(2,1)} %bitcast.155), kind=kOutput, calls=%fused_computation.2 | convolution fusion | flops 1610612736 | bytes 15990784 | tf_op jit(solution)/shard_map/td,rd->tr/dot_general | solution.py:891
  106.8 2.6 stack.25
  109.6 5.7 %fusion.18 = bf16[3,4096]{1,0:T(4,128)(2,1)S(1)} fusion(bf16[3,1024]{1,0:T(4,128)(2,1)} %collective-permute-done, bf16[8192,1024]{1,0:T(8,128)(2,1)} %bitcast.156), kind=kOutput, calls=%fused_computation.22 | convolution fusion | flops 25178112 | bytes 8421376 | tf_op jit(solution)/shard_map/td,rd->tr/dot_general | solution.py:892
  115.9 3.1 fusion.32
  119.0 9.7 %shard_map.228 = (f32[1,8,128,128]{3,2,1,0:T(8,128)S(1)}, f32[128,1024]{1,0:T(8,128)S(1)}, f32[128,2048]{1,0:T(8,128)S(1)}, f32[128,1024]{1,0:T(8,128)S(1)}, f32...) custom-call(f32[128,4096]{1,0:T(8,128)} %get-tuple-element.87.q_ref.k_ref.v_ref, ...), custom_call_target="tpu_custom_call" | custom-call | tf_op jit(solution)/shard_map/pallas_call | solution.py:243
  129.7 3.4 collective-permute-start.5
  140.0 2.8 collective-permute-start.6
  144.8 83.1 %shard_map.230 = bf16[32,264,1024]{2,1,0:T(8,128)(2,1)} custom-call(bf16[264,1024]{1,0:T(8,128)(2,1)} %convert_element_type.110.shard_ref), custom_call_target="tpu_custom_call" | custom-call | tf_op jit(solution)/shard_map/pallas_call | solution.py:562
  228.7 3.5 collective-permute-start.1
  234.8 2.6 convolution_add_fusion.4
  242.1 3.2 multiply_reduce_fusion.6
  245.5 6.8 %fusion.6 = f32[128,5632]{1,0:T(8,128)S(1)} fusion(bf16[128,1024]{1,0:T(8,128)(2,1)S(1)} %multiply_convert_fusion.3, bf16[8448,1024]{1,0:T(8,128)(2,1)} %bitcast.162), kind=kOutput, calls=%fused_computation.6 | convolution fusion | flops 1476395008 | bytes 14680064 | tf_op jit(solution)/shard_map/td,rd->tr/dot_general | solution.py:994
  252.2 4.9 multiply_convert_fusion.1
  257.2 6.0 %multiply_reduce_fusion.4 = (f32[1024]{0:T(1024)}, f32[128]{0:T(128)S(1)}, f32[128,1024]{1,0:T(8,128)S(1)}) fusion(f32[128,1024]{1,0:T(8,128)S(1)} %get-tuple-element.120, f32[128]{0:T(128)S(1)} %get-tuple-element.118, f32[1024]{0:T(1024)S(1)} %get-tuple-element.96, bf16[8448,1024]{1,0:T(8,128)(2,1)} %bitcast.164, ...), kind=kOutput, calls=%fused_computation.103 | convolution fusion | flops 1480063872 | bytes 14033920 | tf_op jit(solution)/shard_map/dot_general | solution.py:1009
  264.1 3.8 fusion.26.mix_ref
  267.9 2.5 shard_map.231
  276.2 4.3 fusion.44
  280.6 8.1 %fusion.21 = bf16[8448,256]{0,1:T(8,128)(2,1)} fusion(bf16[2816,128]{0,1:T(8,128)(2,1)S(1)} %bitcast.168, bf16[5632,128]{0,1:T(8,128)(2,1)S(1)} %fusion.51), kind=kLoop, calls=%fused_computation.23 | loop fusion | flops 17301504 | bytes 6488064 | tf_op jit(solution)/shard_map/concatenate | solution.py:825
  288.7 6.4 %copy.165 = bf16[8448,256]{1,0:T(8,128)(2,1)} copy(bf16[8448,256]{0,1:T(8,128)(2,1)} %fusion.21) | data formatting | bytes 8650752 | tf_op jit(solution)/shard_map/concatenate | solution.py:825
  295.1 86.1 %shard_map.234 = f32[264,1024]{1,0:T(8,128)} custom-call(bf16[32,264,256]{2,1,0:T(8,128)(2,1)} %bitcast.166, bf16[256,1024]{1,0:T(8,128)(2,1)} %pad_maximum_fusion.5.refs_1_), custom_call_target="tpu_custom_call" | custom-call | tf_op jit(solution)/shard_map/pallas_call | solution.py:794
  381.3 3.7 multiply_subtract_fusion
  390.8 5.8 %collective-permute-done.7 = bf16[8,128,128]{2,1,0:T(8,128)(2,1)S(1)} collective-permute-done((bf16[8,128,128]{2,1,0:T(8,128)(2,1)}, bf16[8,128,128]{2,1,0:T(8,128)(2,1)S(1)}, u32[]{:S(2)}, u32[]{:S(2)}) %collective-permute-start.7) | collective-permute-done | bytes 262176 | tf_op jit(solution)/shard_map/ppermute | solution.py:37
  396.6 2.4 fusion.33.next_ref
  400.0 7.8 %shard_map.232 = (f32[128,1024]{1,0:T(8,128)S(1)}, f32[128,1024]{1,0:T(8,128)S(1)}, f32[128,2048]{1,0:T(8,128)S(1)}, f32[8,1,8,128]{3,2,1,0:T(8,128)S(1)}, f32[8,1,128,8]{3,2,1,0:T(8,128)S(1)}) custom-call(f32[128,4096]{1,0:T(8,128)} %get-tuple-element.87.q_ref.k_ref.v_ref, f32[128,4096]{1,0:T(8,128)} %get-tuple-element.87.q_ref.k_ref.v_ref, ...), custom_call_target="tpu_custom_call" | custom-call | tf_op jit(solution)/shard_map/pallas_call | solution.py:243
  415.9 2.4 multiply_reduce_fusion.3
  422.4 3.9 collective-permute-done.13
  428.5 7.1 %fusion.22 = bf16[8192,256]{0,1:T(8,128)(2,1)} fusion(bf16[2048,128]{0,1:T(8,128)(2,1)S(1)} %bitcast.152, bf16[6144,128]{0,1:T(8,128)(2,1)S(1)} %fusion.52), kind=kLoop, calls=%fused_computation.24 | loop fusion | flops 16777216 | bytes 6291456 | tf_op jit(solution)/shard_map/concatenate | solution.py:825
  435.7 6.4 %copy.164 = bf16[8192,256]{1,0:T(8,128)(2,1)} copy(bf16[8192,256]{0,1:T(8,128)(2,1)} %fusion.22) | data formatting | bytes 8388608 | tf_op jit(solution)/shard_map/concatenate | solution.py:825
  442.8 91.9 %shard_map.233 = (f32[256,1024]{1,0:T(8,128)}, f32[4,280,128]{2,1,0:T(8,128)}) custom-call(bf16[32,256,256]{2,1,0:T(8,128)(2,1)} %bitcast.167, bf16[256,1024]{1,0:T(8,128)(2,1)} %pad_maximum_fusion.4.refs_1_, f32[280,128]{1,0:T(8,128)} %pad_bitcast_fusion.refs_2_), custom_call_target="tpu_custom_call" | custom-call | tf_op jit(solution)/shard_map/pallas_call | solution.py:794
  535.7 3.6 multiply_subtract_fusion.1
  (254 shorter events, 72.6 us)
Async XLA Ops:
  0.7 15.1 %copy-start.26 = (f32[256,1024]{1,0:T(8,128)S(1)}, f32[256,1024]{1,0:T(8,128)}, u32[]{:S(2)}) copy-start(f32[256,1024]{1,0:T(8,128)} %param.15) | copy-start | bytes 3145732
  1.5 95.6 %copy-start.46 = (f32[1024]{0:T(1024)}, f32[1024]{0:T(1024)S(1)}, u32[]{:S(2)}) copy-start(f32[1024]{0:T(1024)S(1)} %get-tuple-element.97) | copy-start | bytes 12292
  3.2 93.9 %copy-start.60 = (f32[128]{0:T(128)}, f32[128]{0:T(128)S(1)}, u32[]{:S(2)}) copy-start(f32[128]{0:T(128)S(1)} %get-tuple-element.116) | copy-start | bytes 1540
  5.0 104.5 %collective-permute-start = (bf16[3,1024]{1,0:T(4,128)(2,1)}, bf16[3,1024]{1,0:T(4,128)(2,1)}, u32[]{:S(2)}, u32[]{:S(2)}) collective-permute-start(bf16[3,1024]{1,0:T(4,128)(2,1)} %slice.186), channel_id=1, source_target_pairs={{0,1},{1,2},{2,3},{4,5},{5,6},{6,7},{8,9},{9,10},{10,11},{12,13},{... | collective-permute-start | bytes 18440 | tf_op jit(solution)/shard_map/ppermute | solution.py:37
  11.2 104.3 %copy-start.40 = (f32[4096]{0:T(1024)}, f32[4096]{0:T(1024)S(1)}, u32[]{:S(2)}) copy-start(f32[4096]{0:T(1024)S(1)} %get-tuple-element.103) | copy-start | bytes 49156
  14.9 82.6 %copy-start.68 = (f32[8]{0:T(128)}, f32[8]{0:T(128)S(1)}, u32[]{:S(2)}) copy-start(f32[8]{0:T(128)S(1)} %get-tuple-element.98) | copy-start | bytes 100
  14.9 82.6 %copy-start.70 = (f32[8]{0:T(128)}, f32[8]{0:T(128)S(1)}, u32[]{:S(2)}) copy-start(f32[8]{0:T(128)S(1)} %get-tuple-element.99) | copy-start | bytes 100
  128.7 15.4 %copy-start.2 = (f32[128,2048]{1,0:T(8,128)}, f32[128,2048]{1,0:T(8,128)S(1)}, u32[]{:S(2)}) copy-start(f32[128,2048]{1,0:T(8,128)S(1)} %get-tuple-element.45.u_ref) | copy-start | bytes 3145732
  128.7 15.4 %copy-start.5 = (f32[128,2048]{1,0:T(8,128)}, f32[128,2048]{1,0:T(8,128)S(1)}, u32[]{:S(2)}) copy-start(f32[128,2048]{1,0:T(8,128)S(1)} %get-tuple-element.38.o_ref) | copy-start | bytes 3145732
  128.7 15.4 %copy-start.9 = (f32[1,8,128,128]{3,2,1,0:T(8,128)}, f32[1,8,128,128]{3,2,1,0:T(8,128)S(1)}, u32[]{:S(2)}) copy-start(f32[1,8,128,128]{3,2,1,0:T(8,128)S(1)} %get-tuple-element.43.inverse_ref) | copy-start | bytes 1572868
  128.7 15.4 %copy-start.11 = (f32[128,1024]{1,0:T(8,128)}, f32[128,1024]{1,0:T(8,128)S(1)}, u32[]{:S(2)}) copy-start(f32[128,1024]{1,0:T(8,128)S(1)} %get-tuple-element.44.w_ref) | copy-start | bytes 1572868
  129.7 103.7 %collective-permute-start.5 = (bf16[8,128,256]{2,1,0:T(8,128)(2,1)}, bf16[8,128,256]{2,1,0:T(8,128)(2,1)}, u32[]{:S(2)}, u32[]{:S(2)}) collective-permute-start(bf16[8,128,256]{2,1,0:T(8,128)(2,1)} %convert_bitcast_fusion.1), channel_id=1, source_target_pairs={{0,2},{1,3},{4,6},{5,7},{8,10},{9,11},{12,14},{13,15},{16,18},{17,... | collective-permute-start | bytes 1572872 | tf_op jit(solution)/shard_map/ppermute | solution.py:37
  133.1 101.7 %collective-permute-start.4 = (bf16[8,128,256]{2,1,0:T(8,128)(2,1)}, bf16[8,128,256]{2,1,0:T(8,128)(2,1)}, u32[]{:S(2)}, u32[]{:S(2)}) collective-permute-start(bf16[8,128,256]{2,1,0:T(8,128)(2,1)} %convert_bitcast_fusion.1), channel_id=1, source_target_pairs={{0,3},{4,7},{8,11},{12,15},{16,19},{20,23},{24,27},{28,31}} | collective-permute-start | bytes 1572872 | tf_op jit(solution)/shard_map/ppermute | solution.py:37
  136.0 92.7 %collective-permute-start.2 = (bf16[8,128,128]{2,1,0:T(8,128)(2,1)}, bf16[8,128,128]{2,1,0:T(8,128)(2,1)}, u32[]{:S(2)}, u32[]{:S(2)}) collective-permute-start(bf16[8,128,128]{2,1,0:T(8,128)(2,1)} %convert_bitcast_fusion.2), channel_id=1, source_target_pairs={{0,2},{1,3},{4,6},{5,7},{8,10},{9,11},{12,14},{13,15},{16,18},{17,... | collective-permute-start | bytes 786440 | tf_op jit(solution)/shard_map/ppermute | solution.py:37
  138.0 94.2 %collective-permute-start.3 = (bf16[8,128,128]{2,1,0:T(8,128)(2,1)}, bf16[8,128,128]{2,1,0:T(8,128)(2,1)}, u32[]{:S(2)}, u32[]{:S(2)}) collective-permute-start(bf16[8,128,128]{2,1,0:T(8,128)(2,1)} %convert_bitcast_fusion.2), channel_id=1, source_target_pairs={{0,3},{4,7},{8,11},{12,15},{16,19},{20,23},{24,27},{28,31}} | collective-permute-start | bytes 786440 | tf_op jit(solution)/shard_map/ppermute | solution.py:37
  140.0 97.4 %collective-permute-start.6 = (bf16[8,128,256]{2,1,0:T(8,128)(2,1)}, bf16[8,128,256]{2,1,0:T(8,128)(2,1)}, u32[]{:S(2)}, u32[]{:S(2)}) collective-permute-start(bf16[8,128,256]{2,1,0:T(8,128)(2,1)} %convert_bitcast_fusion.1), channel_id=1, source_target_pairs={{0,1},{1,2},{2,3},{4,5},{5,6},{6,7},{8,9},{9,10},{10,11},{12,13},{... | collective-permute-start | bytes 1572872 | tf_op jit(solution)/shard_map/ppermute | solution.py:37
  144.1 94.8 %copy-start.1 = (f32[128,2048]{1,0:T(8,128)}, f32[128,2048]{1,0:T(8,128)S(1)}, u32[]{:S(2)}) copy-start(f32[128,2048]{1,0:T(8,128)S(1)} %slice.194.gate_ref) | copy-start | bytes 3145732
  144.8 83.1 %copy-start.30 = (f32[1,128,1024]{2,1,0:T(8,128)S(1)}, f32[1,128,1024]{2,1,0:T(8,128)}, u32[]{:S(2)}) copy-start(f32[1,128,1024]{2,1,0:T(8,128)} %param.14) | copy-start | bytes 1572868
  228.7 8.6 %collective-permute-start.1 = (bf16[8,128,128]{2,1,0:T(8,128)(2,1)}, bf16[8,128,128]{2,1,0:T(8,128)(2,1)}, u32[]{:S(2)}, u32[]{:S(2)}) collective-permute-start(bf16[8,128,128]{2,1,0:T(8,128)(2,1)} %convert_bitcast_fusion.2), channel_id=1, source_target_pairs={{0,1},{1,2},{2,3},{4,5},{5,6},{6,7},{8,9},{9,10},{10,11},{12,13},{... | collective-permute-start | bytes 786440 | tf_op jit(solution)/shard_map/ppermute | solution.py:37
  232.2 155.1 %collective-permute-start.8 = (bf16[8,128,128]{2,1,0:T(8,128)(2,1)}, bf16[8,128,128]{2,1,0:T(8,128)(2,1)}, u32[]{:S(2)}, u32[]{:S(2)}) collective-permute-start(bf16[8,128,128]{2,1,0:T(8,128)(2,1)} %convert_bitcast_fusion.2), channel_id=1, source_target_pairs={{2,0},{3,1},{6,4},{7,5},{10,8},{11,9},{14,12},{15,13},{18,16},{19,... | collective-permute-start | bytes 786440 | tf_op jit(solution)/shard_map/ppermute | solution.py:37
  233.4 155.4 %collective-permute-start.9 = (bf16[8,128,128]{2,1,0:T(8,128)(2,1)}, bf16[8,128,128]{2,1,0:T(8,128)(2,1)}, u32[]{:S(2)}, u32[]{:S(2)}) collective-permute-start(bf16[8,128,128]{2,1,0:T(8,128)(2,1)} %convert_bitcast_fusion.2), channel_id=1, source_target_pairs={{3,0},{7,4},{11,8},{15,12},{19,16},{23,20},{27,24},{31,28}} | collective-permute-start | bytes 786440 | tf_op jit(solution)/shard_map/ppermute | solution.py:37
  271.4 117.5 %collective-permute-start.11 = (bf16[8,128,256]{2,1,0:T(8,128)(2,1)}, bf16[8,128,256]{2,1,0:T(8,128)(2,1)}, u32[]{:S(2)}, u32[]{:S(2)}) collective-permute-start(bf16[8,128,256]{2,1,0:T(8,128)(2,1)} %convert_bitcast_fusion), channel_id=1, source_target_pairs={{2,0},{3,1},{6,4},{7,5},{10,8},{11,9},{14,12},{15,13},{18,16},{19,... | collective-permute-start | bytes 1572872 | tf_op jit(solution)/shard_map/ppermute | solution.py:37
  272.7 116.2 %collective-permute-start.10 = (bf16[8,128,256]{2,1,0:T(8,128)(2,1)}, bf16[8,128,256]{2,1,0:T(8,128)(2,1)}, u32[]{:S(2)}, u32[]{:S(2)}) collective-permute-start(bf16[8,128,256]{2,1,0:T(8,128)(2,1)} %convert_bitcast_fusion), channel_id=1, source_target_pairs={{3,0},{7,4},{11,8},{15,12},{19,16},{23,20},{27,24},{31,28}} | collective-permute-start | bytes 1572872 | tf_op jit(solution)/shard_map/ppermute | solution.py:37
  274.0 122.6 %collective-permute-start.12 = (bf16[8,128,256]{2,1,0:T(8,128)(2,1)}, bf16[8,128,256]{2,1,0:T(8,128)(2,1)}, u32[]{:S(2)}, u32[]{:S(2)}) collective-permute-start(bf16[8,128,256]{2,1,0:T(8,128)(2,1)} %convert_bitcast_fusion), channel_id=1, source_target_pairs={{1,0},{2,1},{3,2},{5,4},{6,5},{7,6},{9,8},{10,9},{11,10},{13,12},{... | collective-permute-start | bytes 1572872 | tf_op jit(solution)/shard_map/ppermute | solution.py:37
  295.1 86.1 %copy-start.25 = (f32[264,1024]{1,0:T(8,128)S(1)}, f32[264,1024]{1,0:T(8,128)}, u32[]{:S(2)}) copy-start(f32[264,1024]{1,0:T(8,128)} %param.18) | copy-start | bytes 3244036
  295.1 86.2 %copy-start.32 = (f32[264,1024]{1,0:T(8,128)S(1)}, f32[264,1024]{1,0:T(8,128)}, u32[]{:S(2)}) copy-start(f32[264,1024]{1,0:T(8,128)} %param.19) | copy-start | bytes 3244036
  295.1 86.2 %copy-start.33 = (f32[264,1024]{1,0:T(8,128)S(1)}, f32[264,1024]{1,0:T(8,128)}, u32[]{:S(2)}) copy-start(f32[264,1024]{1,0:T(8,128)} %param.20) | copy-start | bytes 3244036
  387.3 9.3 %collective-permute-start.7 = (bf16[8,128,128]{2,1,0:T(8,128)(2,1)}, bf16[8,128,128]{2,1,0:T(8,128)(2,1)S(1)}, u32[]{:S(2)}, u32[]{:S(2)}) collective-permute-start(bf16[8,128,128]{2,1,0:T(8,128)(2,1)} %convert_bitcast_fusion.2), channel_id=1, source_target_pairs={{1,0},{2,1},{3,2},{5,4},{6,5},{7,6},{9,8},{10,9},{11,10},{13,12},{... | collective-permute-start | bytes 786440 | tf_op jit(solution)/shard_map/ppermute | solution.py:37
  420.1 6.1 %collective-permute-start.13 = (bf16[3,4096]{1,0:T(4,128)(2,1)S(1)}, bf16[3,4096]{1,0:T(4,128)(2,1)S(1)}, u32[]{:S(2)}, u32[]{:S(2)}) collective-permute-start(bf16[3,4096]{1,0:T(4,128)(2,1)S(1)} %slice.201), channel_id=1, source_target_pairs={{1,0},{2,1},{3,2},{5,4},{6,5},{7,6},{9,8},{10,9},{11,10},{13,12},{... | collective-permute-start | bytes 73736 | tf_op jit(solution)/shard_map/ppermute | solution.py:37
  442.8 92.8 %copy-start.27 = (f32[256,1024]{1,0:T(8,128)S(1)}, f32[256,1024]{1,0:T(8,128)}, u32[]{:S(2)}) copy-start(f32[256,1024]{1,0:T(8,128)} %param.15) | copy-start | bytes 3145732
  442.8 92.8 %copy-start.34 = (f32[256,1024]{1,0:T(8,128)S(1)}, f32[256,1024]{1,0:T(8,128)}, u32[]{:S(2)}) copy-start(f32[256,1024]{1,0:T(8,128)} %param.16) | copy-start | bytes 3145732
  442.8 92.8 %copy-start.35 = (f32[256,1024]{1,0:T(8,128)S(1)}, f32[256,1024]{1,0:T(8,128)}, u32[]{:S(2)}) copy-start(f32[256,1024]{1,0:T(8,128)} %param.17) | copy-start | bytes 3145732
  (58 other events, 242.2 us)

commit v2 on v1

--- a/solution.py
+++ b/solution.py
@@ -654,29 +654,54 @@
     return (send, finish, close)
 
 
-def scatter_kernel(extents, parts, order, small, *refs):
+def scatter_kernel(extents, parts, order, small, border, *refs):
     left_ref, right_ref, refs = (refs[0], refs[1], refs[2:])
     if small:
         small_ref, out_ref, total_ref, refs = (refs[0], refs[1], refs[2], refs[3:])
     else:
         out_ref, refs = (refs[0], refs[1:])
     count = len(parts)
-    stages, sides, rooms, accs = [refs[i * count : (i + 1) * count] for i in range(4)]
-    side_got, child_got, side_sent, sent = refs[4 * count : 4 * count + 4]
+    stages, sides, owns, rooms, accs = [refs[i * count : (i + 1) * count] for i in range(5)]
+    side_got, child_got, side_sent, sent = refs[5 * count : 5 * count + 4]
     place = Place(extents)
     chips = extents["z"] * extents["y"] * extents["x"]
+    high, columns = (left_ref.shape[1], right_ref.shape[1])
     rank = {}
     for part, (_, _, dims) in enumerate(parts):
         for slot in route_slots(dims, extents):
             rank[part, slot_key(slot)] = len(rank)
     place.greet(whole=small)
     if small:
-        send, finish, close = small_steps(place, small_ref, total_ref, *refs[4 * count + 4 :])
+        send, finish, close = small_steps(place, small_ref, total_ref, *refs[5 * count + 4 :])
         send(0)
 
-    def product(slot, part, core):
-        start, rows, _ = parts[part]
-        return dot(left_ref[place.shard_index(slot, core), pl.ds(start, rows)], right_ref[...])
+    def product(shard):
+        left = left_ref[shard].astype(jnp.float32)
+        line = lax.broadcasted_iota(jnp.int32, (high, 1), 0) + shard * high
+        early = jnp.where(line < border, 1.0, 0.0)
+        wide = jnp.concatenate([left * early, left * (1.0 - early)], axis=1)
+        return dot(wide.astype(jnp.bfloat16), right_ref[...]).astype(jnp.bfloat16)
+
+    def spread(turn, carry):
+        z = (place.z + extents["z"] // 2 + turn // 4) % extents["z"]
+        y = (place.y + 1 + (turn // 2) % 2) % 2
+        x = (place.x + 1 + turn % 2) % 2
+        chip = (z * 2 + y) * 2 + x
+        theirs = product(((z * 2 + 1 - place.core) * 2 + y) * 2 + x)
+        for part, (start, rows, _) in enumerate(parts):
+            stages[part][chip] = theirs[start : start + rows]
+            pltpu.make_async_remote_copy(
+                src_ref=stages[part].at[chip],
+                dst_ref=sides[part].at[chip],
+                send_sem=side_sent.at[part],
+                recv_sem=side_got.at[part, chip],
+                device_id=place.neighbour("core", 0),
+                device_id_type=MESH,
+            ).start()
+        mine = product(((z * 2 + place.core) * 2 + y) * 2 + x)
+        for part, (start, rows, _) in enumerate(parts):
+            owns[part][chip] = mine[start : start + rows]
+        return carry
 
     def room_index(part, slot, dim, side):
         z, y, x = place.source(slot)
@@ -687,23 +712,12 @@
             index = index * extents[name] + spot[name]
         return base + index
 
-    def hand_over(part, key):
-        slot = dict(zip(("z", "y", "x"), key))
-
-        def step():
-            chip = place.chip_index(slot)
-            stage = stages[part].at[chip]
-            stage[...] = product(slot, part, 1 - place.core).astype(jnp.bfloat16)
-            pltpu.make_async_remote_copy(
-                src_ref=stage,
-                dst_ref=sides[part].at[chip],
-                send_sem=side_sent.at[part],
-                recv_sem=side_got.at[rank[part, key]],
-                device_id=place.neighbour("core", 0),
-                device_id_type=MESH,
-            ).start()
-
-        guarded(place.valid(slot), step)
+    def by_columns(body):
+        def one(turn, carry):
+            body(pl.ds(pl.multiple_of(turn * 128, 128), 128))
+            return carry
+
+        lax.fori_loop(0, columns // 128, one, 0)
 
     def merge(part, key):
         start, rows, dims = parts[part]
@@ -711,24 +725,61 @@
         number = rank[part, key]
 
         def step():
-            side = sides[part].at[place.chip_index(slot)]
-            acc = accs[part]
-            acc[...] = product(slot, part, place.core)
-            drain(side, side_got.at[number])
-            acc[...] += side[...].astype(jnp.float32)
-            for dim, sign, _ in route_children(slot, dims, extents):
-                room = rooms[part].at[room_index(part, slot, dim, sign)]
-                got = child_got.at[number, CHILD_SEM[dim, sign]]
+            chip = place.chip_index(slot)
+            side, own, acc = (sides[part].at[chip], owns[part].at[chip], accs[part])
+            found = [
+                (
+                    rooms[part].at[room_index(part, slot, dim, sign)],
+                    child_got.at[number, CHILD_SEM[dim, sign]],
+                    place.has(dim, sign),
+                )
+                for dim, sign, _ in route_children(slot, dims, extents)
+            ]
+            sure = [room for room, _, near in found if near is None]
+            maybe = [one for one in found if one[2] is not None]
+            drain(side, side_got.at[part, chip])
+            for room, got, near in found:
+                if near is None:
+                    drain(room, got)
+            last = key == (0, 0, 0)
+
+            def settle(value, cut):
+                if maybe:
+                    acc[:, cut] = value
+                elif last:
+                    out_ref[pl.ds(start, rows), cut] = value
+                else:
+                    side[:, cut] = value.astype(jnp.bfloat16)
+
+            def base(cut):
+                value = own[:, cut].astype(jnp.float32) + side[:, cut].astype(jnp.float32)
+                for room in sure:
+                    value = value + room[:, cut].astype(jnp.float32)
+                settle(value, cut)
+
+            by_columns(base)
+            for room, got, near in maybe:
 
                 def take(room=room, got=got):
                     drain(room, got)
-                    acc[...] += room[...].astype(jnp.float32)
-
-                guarded(place.has(dim, sign), take)
-            if key == (0, 0, 0):
-                out_ref[pl.ds(start, rows)] = acc[...]
+
+                    def more(cut):
+                        acc[:, cut] += room[:, cut].astype(jnp.float32)
+
+                    by_columns(more)
+
+                pl.when(near)(take)
+            if maybe:
+
+                def close_up(cut):
+                    if last:
+                        out_ref[pl.ds(start, rows), cut] = acc[:, cut]
+                    else:
+                        side[:, cut] = acc[:, cut].astype(jnp.bfloat16)
+
+                by_columns(close_up)
+            if last:
                 return
-            side[...] = acc[...].astype(jnp.bfloat16)
             dim, sign, seen, parent = route_parent(slot)(dims)
             pltpu.make_async_remote_copy(
                 src_ref=side,
@@ -741,12 +792,8 @@
 
         guarded(place.valid(slot), step)
 
-    ahead = 8
-    for one in order[:ahead]:
-        hand_over(*one)
+    lax.fori_loop(0, chips, spread, 0)
     for i, one in enumerate(order):
-        if i + ahead < len(order):
-            hand_over(*order[i + ahead])
         merge(*one)
         if small and (i + 1) % (len(order) // 5) == 0 and (i + 1) // (len(order) // 5) <= 4:
             finish((i + 1) // (len(order) // 5) - 1)
@@ -757,7 +804,7 @@
         drain(sides[part].at[pl.ds(0, chips - 1)], sent.at[part])
 
 
-def scattered(left, right, small, extents, number):
+def scattered(left, right, border, small, extents, number):
     total, rows, depth = left.shape
     columns = right.shape[1]
     chips = total // 2
@@ -768,15 +815,14 @@
     args = (left, right)
     outs = [jax.ShapeDtypeStruct((rows, columns), jnp.float32)]
     scratch = (
-        [pltpu.VMEM((chips, size, columns), jnp.bfloat16) for _, size, _ in parts]
-        + [pltpu.VMEM((chips, size, columns), jnp.bfloat16) for _, size, _ in parts]
+        [pltpu.VMEM((chips, size, columns), jnp.bfloat16) for _, size, _ in parts] * 3
         + [
             pltpu.VMEM((child_rooms(dims, extents)[1], size, columns), jnp.bfloat16)
             for _, size, dims in parts
         ]
         + [pltpu.VMEM((size, columns), jnp.float32) for _, size, _ in parts]
         + [
-            pltpu.SemaphoreType.DMA((slots,)),
+            pltpu.SemaphoreType.DMA((len(parts), chips)),
             pltpu.SemaphoreType.DMA((slots, 4)),
             pltpu.SemaphoreType.DMA((len(parts),)),
             pltpu.SemaphoreType.DMA((len(parts),)),
@@ -792,7 +838,7 @@
             pltpu.SemaphoreType.DMA((4, most)),
         ]
     return pl.pallas_call(
-        functools.partial(scatter_kernel, extents, parts, order, small is not None),
+        functools.partial(scatter_kernel, extents, parts, order, small is not None, border),
         out_shape=outs,
         in_specs=[vmem] * len(args),
         out_specs=[vmem] * len(outs),
@@ -821,22 +867,17 @@
     if not routed():
         grad = to_owners(owner_rows(first_left, first_right, second_left, second_right))
         return (grad, None if small is None else lax.psum(small, ("dp", "ctx")))
-    tokens = first_left.shape[0]
-    left = jnp.concatenate(
-        [
-            jnp.pad(first_left.T, ((0, 0), (0, tokens))),
-            jnp.pad(second_left.T, ((0, 0), (tokens, 0))),
-        ]
-    )
+    left = jnp.concatenate([first_left.T, second_left.T])
+    border = first_left.shape[1]
     devices = lax.axis_size("dp") * lax.axis_size("ctx")
-    left = left.reshape(devices, left.shape[0] // devices, 2 * tokens)
+    left = left.reshape(devices, left.shape[0] // devices, left.shape[1])
     right = jnp.concatenate([first_right, second_right])
     if small is None:
-        return (scattered(left, right, None, route_extents(), number)[0], None)
+        return (scattered(left, right, border, None, route_extents(), number)[0], None)
     extent = small.shape[0]
     rows = -(-extent // 1024) * 8
     packed = jnp.pad(small, (0, rows * 128 - extent)).reshape(rows, 128)
-    grad, totals = scattered(left, right, packed, route_extents(), number)
+    grad, totals = scattered(left, right, border, packed, route_extents(), number)
     return (grad, totals[3].reshape(-1)[:extent])
 
 
@@ -888,10 +929,14 @@
     gate_half = gate_rows.astype(jnp.bfloat16)
     logits = jnp.einsum("td,rd->tr", normed, gate_half, preferred_element_type=jnp.float32)
     rim_normed = shifted(normed[token_count - margin :], 1)
-    projected = jnp.einsum("td,rd->tr", normed, in_weight, preferred_element_type=jnp.float32)
-    rim_rows = jnp.einsum(
-        "td,rd->tr", rim_normed, in_weight[:channels], preferred_element_type=jnp.float32
-    ).astype(jnp.bfloat16)
+    projected = jnp.einsum(
+        "td,rd->tr",
+        jnp.concatenate([normed, rim_normed]),
+        in_weight,
+        preferred_element_type=jnp.float32,
+    )
+    rim_rows = projected[token_count:, :channels].astype(jnp.bfloat16)
+    projected = projected[:token_count]
     conv_input = projected[:, :channels].astype(jnp.bfloat16)
     gate_pre = projected[:, channels:]
     extended = jnp.concatenate([rim_rows, conv_input]).astype(jnp.float32)

time: 550 us -> 546 us (level)
  the two profiles are of different devices: /device:TPU:0 before, /device:TPU:21 now
where the time goes in v2:
time: 546 us; the launch traced here: 536 us
  Pallas kernels  370 us (68%)
  matrix products  53.6 us (10%)
  local copies, waits for them, and re-layouts  36.4 us (7%)
  other arithmetic  35.1 us (6%)
  starting transfers between devices  29.8 us (5%)
  waiting for transfers between devices  8.32 us (2%)
    pallas_call x2, Pallas kernels, scattered(): pl.pallas_call(functools.partial(scatter_kernel, extents, parts, order, s...  187 us
    pallas_call x2, Pallas kernels, gathered(): pl.pallas_call(functools.partial(gather_kernel, extents, parts, order), o...  162 us
    ppermute x14, starting transfers between devices, passed_along(): return lax.ppermute(shard, axis, pairs)  29.8 us
    pallas_call x4, Pallas kernels, kernel_call(): pl.pallas_call(body, grid=grid, in_specs=in_specs, out_specs=out_specs, o...  21 us
    unnamed x164, local copies, waits for them, and re-layouts  11.7 us
  transfers between devices with their start and end apart: 14, of which 3 were waited for; matrix products, arithmetic and copies ran while one was open for 13% of the time, Pallas kernels for 48%

profile of v2, /device:TPU:21, one launch (start us, length us, event | category | flops | bytes accessed | tf_op | source)
XLA Modules:
  0.0 535.6 jit_solution(2239897701193488913)
XLA Ops:
  5.0 3.1 collective-permute-start
  18.8 68.6 %shard_map.227 = bf16[32,256,1024]{2,1,0:T(8,128)(2,1)} custom-call(bf16[256,1024]{1,0:T(8,128)(2,1)} %convert_element_type.101.shard_ref), custom_call_target="tpu_custom_call" | custom-call | tf_op jit(solution)/shard_map/pallas_call | solution.py:562
  91.8 2.2 stack.25
  94.2 10.7 %fusion.118 = (bf16[131,6144]{1,0:T(8,128)(2,1)S(1)}, f32[131,6144]{1,0:T(8,128)}) fusion(bf16[8192,1024]{1,0:T(8,128)(2,1)} %bitcast.157, bf16[3,1024]{1,0:T(4,128)(2,1)} %collective-permute-done, bf16[128,1024]{1,0:T(8,128)(2,1)S(1)} %fusion.44), kind=kOutput, calls=%fused_computation.196 | convolution fusion | flops 1649702912 | bytes 17682432 | tf_op jit(solution)/shard_map/td,rd->tr/dot_general | solution.py:932
  105.7 3.1 fusion.21
  108.9 9.7 %shard_map.228 = (f32[1,8,128,128]{3,2,1,0:T(8,128)S(1)}, f32[128,1024]{1,0:T(8,128)S(1)}, f32[128,2048]{1,0:T(8,128)S(1)}, f32[128,1024]{1,0:T(8,128)S(1)}, f32...) custom-call(f32[128,4096]{1,0:T(8,128)} %get-tuple-element.87.q_ref.k_ref.v_ref, ...), custom_call_target="tpu_custom_call" | custom-call | tf_op jit(solution)/shard_map/pallas_call | solution.py:243
  127.7 2.8 collective-permute-start.6
  131.2 93.8 %shard_map.230 = bf16[32,264,1024]{2,1,0:T(8,128)(2,1)} custom-call(bf16[264,1024]{1,0:T(8,128)(2,1)} %convert_element_type.100.shard_ref), custom_call_target="tpu_custom_call" | custom-call | tf_op jit(solution)/shard_map/pallas_call | solution.py:562
  229.0 2.0 collective-permute-start.8
  232.4 2.6 convolution_add_fusion.4
  234.9 2.9 collective-permute-done.1
  242.2 3.2 multiply_reduce_fusion.6
  245.5 6.8 %fusion.6 = f32[128,5632]{1,0:T(8,128)S(1)} fusion(bf16[128,1024]{1,0:T(8,128)(2,1)S(1)} %multiply_convert_fusion.3, bf16[8448,1024]{1,0:T(8,128)(2,1)} %bitcast.153), kind=kOutput, calls=%fused_computation.6 | convolution fusion | flops 1476395008 | bytes 14680064 | tf_op jit(solution)/shard_map/td,rd->tr/dot_general | solution.py:1039
  252.3 4.9 multiply_convert_fusion.1
  257.2 6.0 %multiply_reduce_fusion.4 = (f32[1024]{0:T(1024)}, f32[128]{0:T(128)S(1)}, f32[128,1024]{1,0:T(8,128)S(1)}) fusion(f32[128,1024]{1,0:T(8,128)S(1)} %get-tuple-element.122, f32[128]{0:T(128)S(1)} %get-tuple-element.118, f32[1024]{0:T(1024)S(1)} %get-tuple-element.96, bf16[8448,1024]{1,0:T(8,128)(2,1)} %bitcast.155, ...), kind=kOutput, calls=%fused_computation.91 | convolution fusion | flops 1480063872 | bytes 14033920 | tf_op jit(solution)/shard_map/dot_general | solution.py:1054
  264.3 3.8 fusion.15.mix_ref
  268.1 2.5 shard_map.231
  271.5 2.1 collective-permute-start.11
  277.9 4.3 fusion.33
  283.7 4.2 copy.165
  287.9 88.7 %shard_map.234 = f32[264,1024]{1,0:T(8,128)} custom-call(bf16[32,264,128]{2,1,0:T(8,128)(2,1)} %bitcast.163, bf16[256,1024]{1,0:T(8,128)(2,1)} %pad_maximum_fusion.7.refs_1_), custom_call_target="tpu_custom_call" | custom-call | tf_op jit(solution)/shard_map/pallas_call | solution.py:840
  376.6 3.7 multiply_subtract_fusion
  382.5 3.4 collective-permute-start.7
  387.8 4.8 collective-permute-done.7
  392.6 2.4 fusion.22.next_ref
  396.0 7.8 %shard_map.232 = (f32[128,1024]{1,0:T(8,128)S(1)}, f32[128,1024]{1,0:T(8,128)S(1)}, f32[128,2048]{1,0:T(8,128)S(1)}, f32[8,1,8,128]{3,2,1,0:T(8,128)S(1)}, f32[8,1,128,8]{3,2,1,0:T(8,128)S(1)}) custom-call(f32[128,4096]{1,0:T(8,128)} %get-tuple-element.87.q_ref.k_ref.v_ref, f32[128,4096]{1,0:T(8,128)} %get-tuple-element.87.q_ref.k_ref.v_ref, ...), custom_call_target="tpu_custom_call" | custom-call | tf_op jit(solution)/shard_map/pallas_call | solution.py:243
  412.4 2.4 multiply_reduce_fusion.3
  416.7 4.3 collective-permute-start.13
  422.4 2.7 fusion.51
  425.3 2.5 copy.164
  428.6 98.3 %shard_map.233 = (f32[256,1024]{1,0:T(8,128)}, f32[4,280,128]{2,1,0:T(8,128)}) custom-call(bf16[32,256,128]{2,1,0:T(8,128)(2,1)} %bitcast.164, bf16[256,1024]{1,0:T(8,128)(2,1)} %pad_maximum_fusion.6.refs_1_, f32[280,128]{1,0:T(8,128)} %pad_bitcast_fusion.refs_2_), custom_call_target="tpu_custom_call" | custom-call | tf_op jit(solution)/shard_map/pallas_call | solution.py:840
  527.9 3.6 multiply_subtract_fusion.1
  (260 shorter events, 69.8 us)
Async XLA Ops:
  0.6 16.4 %copy-start.24 = (f32[264,1024]{1,0:T(8,128)S(1)}, f32[264,1024]{1,0:T(8,128)}, u32[]{:S(2)}) copy-start(f32[264,1024]{1,0:T(8,128)} %param.18) | copy-start | bytes 3244036
  0.7 17.3 %copy-start.25 = (f32[256,1024]{1,0:T(8,128)S(1)}, f32[256,1024]{1,0:T(8,128)}, u32[]{:S(2)}) copy-start(f32[256,1024]{1,0:T(8,128)} %param.15) | copy-start | bytes 3145732
  3.3 11.3 %copy-start.63 = (f32[128]{0:T(128)}, f32[128]{0:T(128)S(1)}, u32[]{:S(2)}) copy-start(f32[128]{0:T(128)S(1)} %get-tuple-element.116) | copy-start | bytes 1540
  5.0 89.1 %collective-permute-start = (bf16[3,1024]{1,0:T(4,128)(2,1)}, bf16[3,1024]{1,0:T(4,128)(2,1)}, u32[]{:S(2)}, u32[]{:S(2)}) collective-permute-start(bf16[3,1024]{1,0:T(4,128)(2,1)} %slice.189), channel_id=1, source_target_pairs={{0,1},{1,2},{2,3},{4,5},{5,6},{6,7},{8,9},{9,10},{10,11},{12,13},{... | collective-permute-start | bytes 18440 | tf_op jit(solution)/shard_map/ppermute | solution.py:37
  9.6 95.8 %copy-start.41 = (f32[4096]{0:T(1024)}, f32[4096]{0:T(1024)S(1)}, u32[]{:S(2)}) copy-start(f32[4096]{0:T(1024)S(1)} %get-tuple-element.100) | copy-start | bytes 49156
  9.6 95.8 %copy-start.43 = (f32[4096]{0:T(1024)}, f32[4096]{0:T(1024)S(1)}, u32[]{:S(2)}) copy-start(f32[4096]{0:T(1024)S(1)} %get-tuple-element.101) | copy-start | bytes 49156
  12.7 74.8 %copy-start.73 = (f32[8]{0:T(128)}, f32[8]{0:T(128)S(1)}, u32[]{:S(2)}) copy-start(f32[8]{0:T(128)S(1)} %get-tuple-element.99) | copy-start | bytes 100
  14.6 72.9 %copy-start.51 = (f32[128,16]{0,1:T(8,128)}, f32[128,16]{0,1:T(8,128)S(1)}, u32[]{:S(2)}) copy-start(f32[128,16]{0,1:T(8,128)S(1)} %fusion.60) | copy-start | bytes 24580
  17.0 70.5 %copy-start.61 = (pred[128]{0:T(512)(128)(4,1)}, pred[128]{0:T(512)(128)(4,1)S(1)}, u32[]{:S(2)}) copy-start(pred[128]{0:T(512)(128)(4,1)S(1)} %get-tuple-element.108) | copy-start | bytes 388
  17.0 70.5 %copy-start.67 = (pred[128]{0:T(512)(128)(4,1)}, pred[128]{0:T(512)(128)(4,1)S(1)}, u32[]{:S(2)}) copy-start(pred[128]{0:T(512)(128)(4,1)S(1)} %get-tuple-element.109) | copy-start | bytes 388
  121.5 109.5 %collective-permute-start.5 = (bf16[8,128,256]{2,1,0:T(8,128)(2,1)}, bf16[8,128,256]{2,1,0:T(8,128)(2,1)}, u32[]{:S(2)}, u32[]{:S(2)}) collective-permute-start(bf16[8,128,256]{2,1,0:T(8,128)(2,1)} %convert_bitcast_fusion.1), channel_id=1, source_target_pairs={{0,2},{1,3},{4,6},{5,7},{8,10},{9,11},{12,14},{13,15},{16,18},{17,... | collective-permute-start | bytes 1572872 | tf_op jit(solution)/shard_map/ppermute | solution.py:37
  122.7 109.6 %collective-permute-start.4 = (bf16[8,128,256]{2,1,0:T(8,128)(2,1)}, bf16[8,128,256]{2,1,0:T(8,128)(2,1)}, u32[]{:S(2)}, u32[]{:S(2)}) collective-permute-start(bf16[8,128,256]{2,1,0:T(8,128)(2,1)} %convert_bitcast_fusion.1), channel_id=1, source_target_pairs={{0,3},{4,7},{8,11},{12,15},{16,19},{20,23},{24,27},{28,31}} | collective-permute-start | bytes 1572872 | tf_op jit(solution)/shard_map/ppermute | solution.py:37
  125.0 102.0 %collective-permute-start.2 = (bf16[8,128,128]{2,1,0:T(8,128)(2,1)}, bf16[8,128,128]{2,1,0:T(8,128)(2,1)}, u32[]{:S(2)}, u32[]{:S(2)}) collective-permute-start(bf16[8,128,128]{2,1,0:T(8,128)(2,1)} %convert_bitcast_fusion.2), channel_id=1, source_target_pairs={{0,2},{1,3},{4,6},{5,7},{8,10},{9,11},{12,14},{13,15},{16,18},{17,... | collective-permute-start | bytes 786440 | tf_op jit(solution)/shard_map/ppermute | solution.py:37
  126.3 102.7 %collective-permute-start.3 = (bf16[8,128,128]{2,1,0:T(8,128)(2,1)}, bf16[8,128,128]{2,1,0:T(8,128)(2,1)}, u32[]{:S(2)}, u32[]{:S(2)}) collective-permute-start(bf16[8,128,128]{2,1,0:T(8,128)(2,1)} %convert_bitcast_fusion.2), channel_id=1, source_target_pairs={{0,3},{4,7},{8,11},{12,15},{16,19},{20,23},{24,27},{28,31}} | collective-permute-start | bytes 786440 | tf_op jit(solution)/shard_map/ppermute | solution.py:37
  127.7 110.2 %collective-permute-start.6 = (bf16[8,128,256]{2,1,0:T(8,128)(2,1)}, bf16[8,128,256]{2,1,0:T(8,128)(2,1)}, u32[]{:S(2)}, u32[]{:S(2)}) collective-permute-start(bf16[8,128,256]{2,1,0:T(8,128)(2,1)} %convert_bitcast_fusion.1), channel_id=1, source_target_pairs={{0,1},{1,2},{2,3},{4,5},{5,6},{6,7},{8,9},{9,10},{10,11},{12,13},{... | collective-permute-start | bytes 1572872 | tf_op jit(solution)/shard_map/ppermute | solution.py:37
  131.2 93.8 %copy-start.29 = (f32[1,128,1024]{2,1,0:T(8,128)S(1)}, f32[1,128,1024]{2,1,0:T(8,128)}, u32[]{:S(2)}) copy-start(f32[1,128,1024]{2,1,0:T(8,128)} %param.14) | copy-start | bytes 1572868
  227.0 12.5 %copy-start.1 = (f32[128,2048]{1,0:T(8,128)}, f32[128,2048]{1,0:T(8,128)S(1)}, u32[]{:S(2)}) copy-start(f32[128,2048]{1,0:T(8,128)S(1)} %slice.198.gate_ref) | copy-start | bytes 3145732
  227.0 10.8 %collective-permute-start.1 = (bf16[8,128,128]{2,1,0:T(8,128)(2,1)}, bf16[8,128,128]{2,1,0:T(8,128)(2,1)}, u32[]{:S(2)}, u32[]{:S(2)}) collective-permute-start(bf16[8,128,128]{2,1,0:T(8,128)(2,1)} %convert_bitcast_fusion.2), channel_id=1, source_target_pairs={{0,1},{1,2},{2,3},{4,5},{5,6},{6,7},{8,9},{9,10},{10,11},{12,13},{... | collective-permute-start | bytes 786440 | tf_op jit(solution)/shard_map/ppermute | solution.py:37
  229.0 153.5 %collective-permute-start.8 = (bf16[8,128,128]{2,1,0:T(8,128)(2,1)}, bf16[8,128,128]{2,1,0:T(8,128)(2,1)}, u32[]{:S(2)}, u32[]{:S(2)}) collective-permute-start(bf16[8,128,128]{2,1,0:T(8,128)(2,1)} %convert_bitcast_fusion.2), channel_id=1, source_target_pairs={{2,0},{3,1},{6,4},{7,5},{10,8},{11,9},{14,12},{15,13},{18,16},{19,... | collective-permute-start | bytes 786440 | tf_op jit(solution)/shard_map/ppermute | solution.py:37
  231.0 154.9 %collective-permute-start.9 = (bf16[8,128,128]{2,1,0:T(8,128)(2,1)}, bf16[8,128,128]{2,1,0:T(8,128)(2,1)}, u32[]{:S(2)}, u32[]{:S(2)}) collective-permute-start(bf16[8,128,128]{2,1,0:T(8,128)(2,1)} %convert_bitcast_fusion.2), channel_id=1, source_target_pairs={{3,0},{7,4},{11,8},{15,12},{19,16},{23,20},{27,24},{31,28}} | collective-permute-start | bytes 786440 | tf_op jit(solution)/shard_map/ppermute | solution.py:37
  271.5 114.4 %collective-permute-start.11 = (bf16[8,128,256]{2,1,0:T(8,128)(2,1)}, bf16[8,128,256]{2,1,0:T(8,128)(2,1)}, u32[]{:S(2)}, u32[]{:S(2)}) collective-permute-start(bf16[8,128,256]{2,1,0:T(8,128)(2,1)} %convert_bitcast_fusion), channel_id=1, source_target_pairs={{2,0},{3,1},{6,4},{7,5},{10,8},{11,9},{14,12},{15,13},{18,16},{19,... | collective-permute-start | bytes 1572872 | tf_op jit(solution)/shard_map/ppermute | solution.py:37
  273.6 112.4 %collective-permute-start.10 = (bf16[8,128,256]{2,1,0:T(8,128)(2,1)}, bf16[8,128,256]{2,1,0:T(8,128)(2,1)}, u32[]{:S(2)}, u32[]{:S(2)}) collective-permute-start(bf16[8,128,256]{2,1,0:T(8,128)(2,1)} %convert_bitcast_fusion), channel_id=1, source_target_pairs={{3,0},{7,4},{11,8},{15,12},{19,16},{23,20},{27,24},{31,28}} | collective-permute-start | bytes 1572872 | tf_op jit(solution)/shard_map/ppermute | solution.py:37
  275.1 117.5 %collective-permute-start.12 = (bf16[8,128,256]{2,1,0:T(8,128)(2,1)}, bf16[8,128,256]{2,1,0:T(8,128)(2,1)}, u32[]{:S(2)}, u32[]{:S(2)}) collective-permute-start(bf16[8,128,256]{2,1,0:T(8,128)(2,1)} %convert_bitcast_fusion), channel_id=1, source_target_pairs={{1,0},{2,1},{3,2},{5,4},{6,5},{7,6},{9,8},{10,9},{11,10},{13,12},{... | collective-permute-start | bytes 1572872 | tf_op jit(solution)/shard_map/ppermute | solution.py:37
  287.9 88.7 %copy-start.32 = (f32[264,1024]{1,0:T(8,128)S(1)}, f32[264,1024]{1,0:T(8,128)}, u32[]{:S(2)}) copy-start(f32[264,1024]{1,0:T(8,128)} %param.19) | copy-start | bytes 3244036
  287.9 88.7 %copy-start.33 = (f32[264,1024]{1,0:T(8,128)S(1)}, f32[264,1024]{1,0:T(8,128)}, u32[]{:S(2)}) copy-start(f32[264,1024]{1,0:T(8,128)} %param.20) | copy-start | bytes 3244036
  382.5 12.5 %copy-start.3 = (f32[128,2048]{1,0:T(8,128)S(1)}, f32[128,2048]{1,0:T(8,128)}, u32[]{:S(2)}) copy-start(f32[128,2048]{1,0:T(8,128)} %copy-done.2) | copy-start | bytes 3145732
  382.5 12.5 %copy-start.8 = (f32[1,8,128,128]{3,2,1,0:T(8,128)S(1)}, f32[1,8,128,128]{3,2,1,0:T(8,128)}, u32[]{:S(2)}) copy-start(f32[1,8,128,128]{3,2,1,0:T(8,128)} %copy-done.7) | copy-start | bytes 1572868
  382.5 10.1 %collective-permute-start.7 = (bf16[8,128,128]{2,1,0:T(8,128)(2,1)}, bf16[8,128,128]{2,1,0:T(8,128)(2,1)S(1)}, u32[]{:S(2)}, u32[]{:S(2)}) collective-permute-start(bf16[8,128,128]{2,1,0:T(8,128)(2,1)} %convert_bitcast_fusion.2), channel_id=1, source_target_pairs={{1,0},{2,1},{3,2},{5,4},{6,5},{7,6},{9,8},{10,9},{11,10},{13,12},{... | collective-permute-start | bytes 786440 | tf_op jit(solution)/shard_map/ppermute | solution.py:37
  416.7 5.3 collective-permute-start.13
  427.8 100.0 %copy-start.26 = (f32[256,1024]{1,0:T(8,128)S(1)}, f32[256,1024]{1,0:T(8,128)}, u32[]{:S(2)}) copy-start(f32[256,1024]{1,0:T(8,128)} %param.15) | copy-start | bytes 3145732
  427.8 100.0 %copy-start.34 = (f32[256,1024]{1,0:T(8,128)S(1)}, f32[256,1024]{1,0:T(8,128)}, u32[]{:S(2)}) copy-start(f32[256,1024]{1,0:T(8,128)} %param.16) | copy-start | bytes 3145732
  427.9 99.9 %copy-start.35 = (f32[256,1024]{1,0:T(8,128)S(1)}, f32[256,1024]{1,0:T(8,128)}, u32[]{:S(2)}) copy-start(f32[256,1024]{1,0:T(8,128)} %param.17) | copy-start | bytes 3145732
  (61 other events, 188.4 us)

commit v3 on v2

--- a/solution.py
+++ b/solution.py
@@ -605,51 +605,83 @@
     return (rooms, base)
 
 
-def small_steps(place, small_ref, total_ref, room_ref, small_got, small_sent):
-    axes = ["core", "x", "y", "z"]
-    spot = {"core": place.core, "x": place.x, "y": place.y, "z": place.z}
-    count = dict(place.extents, core=2)
-
-    def peer(dim, other):
+def small_steps(place, small_ref, total_ref, *refs):
+    work, half, quarter, eighth, line, got, sent = refs
+    depth = place.extents["z"]
+    fours = place.core * 4
+    twos = fours + place.x * 2
+    one = twos + place.y
+    swaps = [
+        ("core", fours, 4, work, 4 - place.core * 4, half),
+        ("x", twos, 2, work, fours + 2 - place.x * 2, quarter),
+        ("y", one, 1, work, twos + 1 - place.y, eighth),
+        ("z", one, 1, None, None, None),
+        ("y", one, 1, total_ref, twos + 1 - place.y, None),
+        ("x", twos, 2, total_ref, fours + 2 - place.x * 2, None),
+        ("core", fours, 4, total_ref, 4 - place.core * 4, None),
+    ]
+
+    def push(level, source, target, dim):
+        pltpu.make_async_remote_copy(
+            src_ref=source,
+            dst_ref=target,
+            send_sem=sent.at[level],
+            recv_sem=got.at[level],
+            device_id=place.neighbour(dim, 0),
+            device_id_type=MESH,
+        ).start()
+
+    def along(other):
+        return pltpu.make_async_remote_copy(
+            src_ref=line.at[place.z],
+            dst_ref=line.at[place.z],
+            send_sem=sent.at[7 + other],
+            recv_sem=got.at[7 + place.z],
+            device_id=(other * 2 + place.core, place.ctx),
+            device_id_type=MESH,
+        )
+
+    def send(level):
+        dim, low, size, buffer, away, room = swaps[level]
+        if level == 0:
+            work[...] = small_ref[...]
         if dim == "z":
-            return (other * 2 + place.core, place.ctx)
-        return place.neighbour(dim, 0)
-
-    def send(level):
-        dim = axes[level]
-        mine = spot[dim]
-        source = small_ref if level == 0 else total_ref.at[level - 1]
-        room_ref[level, mine] = source[...]
-        for other in range(count[dim]):
-            copy = pltpu.make_async_remote_copy(
-                src_ref=source,
-                dst_ref=room_ref.at[level, mine],
-                send_sem=small_sent.at[level, other],
-                recv_sem=small_got.at[level, mine],
-                device_id=peer(dim, other),
-                device_id_type=MESH,
-            )
-            pl.when(mine != other)(copy.start)
+            line[place.z] = work[one]
+            for other in range(depth):
+                pl.when(place.z != other)(along(other).start)
+        elif room is not None:
+            push(level, buffer.at[pl.ds(away, size)], room, dim)
+        else:
+            push(level, buffer.at[pl.ds(low, size)], buffer.at[pl.ds(low, size)], dim)
 
     def finish(level):
-        dim = axes[level]
-        mine = spot[dim]
-        for other in range(count[dim]):
-            room = room_ref.at[level, other]
-            pl.when(mine != other)(functools.partial(drain, room, small_got.at[level, other]))
-        value = room_ref[level, 0]
-        for other in range(1, count[dim]):
-            value = value + room_ref[level, other]
-        total_ref[level] = value
-        if level + 1 < len(axes):
+        dim, low, size, buffer, away, room = swaps[level]
+        if dim == "z":
+            for other in range(depth):
+                pl.when(place.z != other)(
+                    functools.partial(drain, line.at[other], got.at[7 + other])
+                )
+            value = line[0]
+            for other in range(1, depth):
+                value = value + line[other]
+            total_ref[one] = value
+        elif room is not None:
+            drain(room, got.at[level])
+            work[pl.ds(low, size)] += room[...]
+        else:
+            drain(buffer.at[pl.ds(away, size)], got.at[level])
+        if level + 1 < len(swaps):
             send(level + 1)
 
     def close():
-        for level, dim in enumerate(axes):
-            for other in range(count[dim]):
-                pl.when(spot[dim] != other)(
-                    functools.partial(drain, room_ref.at[level, 0], small_sent.at[level, other])
-                )
+        for level, (dim, _, size, _, _, _) in enumerate(swaps):
+            if dim == "z":
+                for other in range(depth):
+                    pl.when(place.z != other)(
+                        functools.partial(drain, line.at[other], sent.at[7 + other])
+                    )
+            else:
+                drain(work.at[pl.ds(0, size)], sent.at[level])
 
     return (send, finish, close)
 
@@ -675,21 +707,33 @@
         send, finish, close = small_steps(place, small_ref, total_ref, *refs[5 * count + 4 :])
         send(0)
 
-    def product(shard):
+    def fill(shard, chip, targets):
         left = left_ref[shard].astype(jnp.float32)
         line = lax.broadcasted_iota(jnp.int32, (high, 1), 0) + shard * high
         early = jnp.where(line < border, 1.0, 0.0)
-        wide = jnp.concatenate([left * early, left * (1.0 - early)], axis=1)
-        return dot(wide.astype(jnp.bfloat16), right_ref[...]).astype(jnp.bfloat16)
-
-    def spread(turn, carry):
-        z = (place.z + extents["z"] // 2 + turn // 4) % extents["z"]
-        y = (place.y + 1 + (turn // 2) % 2) % 2
-        x = (place.x + 1 + turn % 2) % 2
+        wide = jnp.concatenate([left * early, left * (1.0 - early)], axis=1).astype(jnp.bfloat16)
+
+        def one(turn, carry):
+            cut = pl.ds(pl.multiple_of(turn * 256, 256), 256)
+            value = dot(wide, right_ref[:, cut]).astype(jnp.bfloat16)
+            for part, (start, rows, _) in enumerate(parts):
+                targets[part].at[chip][:, cut] = value[start : start + rows]
+            return carry
+
+        lax.fori_loop(0, columns // 256, one, 0)
+
+    def far_first(z, turn):
+        depth = extents["z"]
+        return depth - 1 - turn if z < depth // 2 else turn
+
+    def spread(turn, flip_y, flip_x):
+        depth = extents["z"]
+        z = jnp.where(place.z < depth // 2, depth - 1 - turn, turn)
+        y = 1 - place.y if flip_y else place.y
+        x = 1 - place.x if flip_x else place.x
         chip = (z * 2 + y) * 2 + x
-        theirs = product(((z * 2 + 1 - place.core) * 2 + y) * 2 + x)
-        for part, (start, rows, _) in enumerate(parts):
-            stages[part][chip] = theirs[start : start + rows]
+        fill(((z * 2 + 1 - place.core) * 2 + y) * 2 + x, chip, stages)
+        for part in range(count):
             pltpu.make_async_remote_copy(
                 src_ref=stages[part].at[chip],
                 dst_ref=sides[part].at[chip],
@@ -698,10 +742,17 @@
                 device_id=place.neighbour("core", 0),
                 device_id_type=MESH,
             ).start()
-        mine = product(((z * 2 + place.core) * 2 + y) * 2 + x)
-        for part, (start, rows, _) in enumerate(parts):
-            owns[part][chip] = mine[start : start + rows]
-        return carry
+        fill(((z * 2 + place.core) * 2 + y) * 2 + x, chip, owns)
+
+    due = {}
+    for z in range(extents["z"]):
+        for turn in range(extents["z"]):
+            ahead = far_first(z, turn) - z
+            for i, (_, key) in enumerate(order):
+                if key[0] == ahead:
+                    name = (turn,) + key[1:]
+                    due[name] = min(due.get(name, i), i)
+    due = sorted((when, name) for name, when in due.items())
 
     def room_index(part, slot, dim, side):
         z, y, x = place.source(slot)
@@ -792,11 +843,13 @@
 
         guarded(place.valid(slot), step)
 
-    lax.fori_loop(0, chips, spread, 0)
+    finishes = [2, 8, 14, 22, 34, 46, 60]
     for i, one in enumerate(order):
+        while due and due[0][0] <= i + 6:
+            spread(*due.pop(0)[1])
         merge(*one)
-        if small and (i + 1) % (len(order) // 5) == 0 and (i + 1) // (len(order) // 5) <= 4:
-            finish((i + 1) // (len(order) // 5) - 1)
+        if small and i * 84 // len(order) in finishes:
+            finish(finishes.index(i * 84 // len(order)))
     if small:
         close()
     for part in range(count):
@@ -830,13 +883,13 @@
     )
     if small is not None:
         args = args + (small,)
-        outs.append(jax.ShapeDtypeStruct((4,) + small.shape, jnp.float32))
-        most = max(2, extents["z"])
+        outs.append(jax.ShapeDtypeStruct(small.shape, jnp.float32))
+        depth = extents["z"]
+        sizes = [8, 4, 2, 1, depth]
         scratch = scratch + [
-            pltpu.VMEM((4, most) + small.shape, jnp.float32),
-            pltpu.SemaphoreType.DMA((4, most)),
-            pltpu.SemaphoreType.DMA((4, most)),
+            pltpu.VMEM((size,) + small.shape[1:], jnp.float32) for size in sizes
         ]
+        scratch = scratch + [pltpu.SemaphoreType.DMA((7 + depth,))] * 2
     return pl.pallas_call(
         functools.partial(scatter_kernel, extents, parts, order, small is not None, border),
         out_shape=outs,
@@ -875,10 +928,10 @@
     if small is None:
         return (scattered(left, right, border, None, route_extents(), number)[0], None)
     extent = small.shape[0]
-    rows = -(-extent // 1024) * 8
-    packed = jnp.pad(small, (0, rows * 128 - extent)).reshape(rows, 128)
+    rows = -(-extent // 8192) * 8
+    packed = jnp.pad(small, (0, rows * 1024 - extent)).reshape(8, rows, 128)
     grad, totals = scattered(left, right, border, packed, route_extents(), number)
-    return (grad, totals[3].reshape(-1)[:extent])
+    return (grad, totals.reshape(-1)[:extent])
 
 
 def shifted(shard, by):

time: 546 us -> 538 us (0.985)
  the two profiles are of different devices: /device:TPU:21 before, /device:TPU:18 now
where the time goes in v3:
time: 538 us; the launch traced here: 527 us
  Pallas kernels  354 us (66%)
  matrix products  53.6 us (10%)
  other arithmetic  36.2 us (7%)
  local copies, waits for them, and re-layouts  35.3 us (7%)
  starting transfers between devices  34.9 us (6%)
  waiting for transfers between devices  10.8 us (2%)
    pallas_call x2, Pallas kernels, scattered(): pl.pallas_call(functools.partial(scatter_kernel, extents, parts, order, s...  180 us
    pallas_call x2, Pallas kernels, gathered(): pl.pallas_call(functools.partial(gather_kernel, extents, parts, order), o...  153 us
    ppermute x14, starting transfers between devices, passed_along(): return lax.ppermute(shard, axis, pairs)  34.9 us
    pallas_call x4, Pallas kernels, kernel_call(): pl.pallas_call(body, grid=grid, in_specs=in_specs, out_specs=out_specs, o...  21 us
    unnamed x174, local copies, waits for them, and re-layouts  11.6 us
    ppermute x14, waiting for transfers between devices, passed_along(): return lax.ppermute(shard, axis, pairs)  10.8 us
  transfers between devices with their start and end apart: 14, of which 3 were waited for; matrix products, arithmetic and copies ran while one was open for 14% of the time, Pallas kernels for 47%

profile of v3, /device:TPU:18, one launch (start us, length us, event | category | flops | bytes accessed | tf_op | source)
XLA Modules:
  0.0 527.2 jit_solution(7232712085467813049)
XLA Ops:
  5.6 3.4 collective-permute-start
  20.2 67.9 %shard_map.227 = bf16[32,256,1024]{2,1,0:T(8,128)(2,1)} custom-call(bf16[256,1024]{1,0:T(8,128)(2,1)} %convert_element_type.101.shard_ref), custom_call_target="tpu_custom_call" | custom-call | tf_op jit(solution)/shard_map/pallas_call | solution.py:562
  92.5 2.2 stack.25
  94.9 10.7 %fusion.118 = (bf16[131,6144]{1,0:T(8,128)(2,1)S(1)}, f32[131,6144]{1,0:T(8,128)}) fusion(bf16[8192,1024]{1,0:T(8,128)(2,1)} %bitcast.155, bf16[3,1024]{1,0:T(4,128)(2,1)} %collective-permute-done, bf16[128,1024]{1,0:T(8,128)(2,1)S(1)} %fusion.44), kind=kOutput, calls=%fused_computation.194 | convolution fusion | flops 1649702912 | bytes 17682432 | tf_op jit(solution)/shard_map/td,rd->tr/dot_general | solution.py:985
  106.3 3.1 fusion.21
  109.4 9.7 %shard_map.228 = (f32[1,8,128,128]{3,2,1,0:T(8,128)S(1)}, f32[128,1024]{1,0:T(8,128)S(1)}, f32[128,2048]{1,0:T(8,128)S(1)}, f32[128,1024]{1,0:T(8,128)S(1)}, f32...) custom-call(f32[128,4096]{1,0:T(8,128)} %get-tuple-element.87.q_ref.k_ref.v_ref, ...), custom_call_target="tpu_custom_call" | custom-call | tf_op jit(solution)/shard_map/pallas_call | solution.py:243
  122.0 3.8 collective-permute-start.5
  131.5 2.4 collective-permute-start.6
  134.5 85.6 %shard_map.230 = bf16[32,264,1024]{2,1,0:T(8,128)(2,1)} custom-call(bf16[264,1024]{1,0:T(8,128)(2,1)} %convert_element_type.100.shard_ref), custom_call_target="tpu_custom_call" | custom-call | tf_op jit(solution)/shard_map/pallas_call | solution.py:562
  222.2 8.7 %collective-permute-start.1 = (bf16[8,128,128]{2,1,0:T(8,128)(2,1)}, bf16[8,128,128]{2,1,0:T(8,128)(2,1)}, u32[]{:S(2)}, u32[]{:S(2)}) collective-permute-start(bf16[8,128,128]{2,1,0:T(8,128)(2,1)} %convert_bitcast_fusion.2), channel_id=1, source_target_pairs={{0,1},{1,2},{2,3},{4,5},{5,6},{6,7},{8,9},{9,10},{10,11},{12,13},{... | collective-permute-start | bytes 786440 | tf_op jit(solution)/shard_map/ppermute | solution.py:37
  233.6 2.6 convolution_add_fusion.4
  241.7 3.2 multiply_reduce_fusion.6
  245.0 6.8 %fusion.6 = f32[128,5632]{1,0:T(8,128)S(1)} fusion(bf16[128,1024]{1,0:T(8,128)(2,1)S(1)} %multiply_convert_fusion.3, bf16[8448,1024]{1,0:T(8,128)(2,1)} %bitcast.151), kind=kOutput, calls=%fused_computation.6 | convolution fusion | flops 1476395008 | bytes 14680064 | tf_op jit(solution)/shard_map/td,rd->tr/dot_general | solution.py:1092
  251.8 4.9 multiply_convert_fusion.1
  256.7 6.0 %multiply_reduce_fusion.4 = (f32[1024]{0:T(1024)}, f32[128]{0:T(128)S(1)}, f32[128,1024]{1,0:T(8,128)S(1)}) fusion(f32[128,1024]{1,0:T(8,128)S(1)} %get-tuple-element.122, f32[128]{0:T(128)S(1)} %get-tuple-element.118, f32[1024]{0:T(1024)S(1)} %copy-done.54, bf16[8448,1024]{1,0:T(8,128)(2,1)} %bitcast.153, bf16[128,2816]{1,0:T(8,128)(2,1)S(1)} %get-tuple-element.90, ...), kind=kOutput, calls=%fused_computation.91 | convolution fusion | flops 1480063872 | bytes 14033920 | tf_op jit(solution)/shard_map/dot_general | solution.py:1107
  263.8 3.8 fusion.15.mix_ref
  267.6 2.5 shard_map.231
  276.6 4.3 fusion.33
  282.4 4.2 copy.165
  286.6 92.4 %shard_map.234 = f32[264,1024]{1,0:T(8,128)} custom-call(bf16[32,264,128]{2,1,0:T(8,128)(2,1)} %bitcast.161, bf16[256,1024]{1,0:T(8,128)(2,1)} %pad_maximum_fusion.7.refs_1_), custom_call_target="tpu_custom_call" | custom-call | tf_op jit(solution)/shard_map/pallas_call | solution.py:893
  379.0 3.7 multiply_subtract_fusion
  385.0 2.3 collective-permute-start.7
  389.1 5.3 %collective-permute-done.7 = bf16[8,128,128]{2,1,0:T(8,128)(2,1)S(1)} collective-permute-done((bf16[8,128,128]{2,1,0:T(8,128)(2,1)}, bf16[8,128,128]{2,1,0:T(8,128)(2,1)S(1)}, u32[]{:S(2)}, u32[]{:S(2)}) %collective-permute-start.7) | collective-permute-done | bytes 262176 | tf_op jit(solution)/shard_map/ppermute | solution.py:37
  394.5 2.4 fusion.22.next_ref
  397.9 7.8 %shard_map.232 = (f32[128,1024]{1,0:T(8,128)S(1)}, f32[128,1024]{1,0:T(8,128)S(1)}, f32[128,2048]{1,0:T(8,128)S(1)}, f32[8,1,8,128]{3,2,1,0:T(8,128)S(1)}, f32[8,1,128,8]{3,2,1,0:T(8,128)S(1)}) custom-call(f32[128,4096]{1,0:T(8,128)} %get-tuple-element.87.q_ref.k_ref.v_ref, f32[128,4096]{1,0:T(8,128)} %get-tuple-element.87.q_ref.k_ref.v_ref, ...), custom_call_target="tpu_custom_call" | custom-call | tf_op jit(solution)/shard_map/pallas_call | solution.py:243
  414.3 2.4 multiply_reduce_fusion.3
  418.6 2.2 collective-permute-start.13
  421.2 4.4 collective-permute-done.13
  425.8 2.7 fusion.51
  428.7 2.5 copy.164
  432.0 87.2 %shard_map.233 = (f32[256,1024]{1,0:T(8,128)}, f32[8,40,128]{2,1,0:T(8,128)}) custom-call(bf16[32,256,128]{2,1,0:T(8,128)(2,1)} %bitcast.162, bf16[256,1024]{1,0:T(8,128)(2,1)} %pad_maximum_fusion.6.refs_1_, f32[8,40,128]{2,1,0:T(8,128)} %bitcast.164), custom_call_target="tpu_custom_call" | custom-call | tf_op jit(solution)/shard_map/pallas_call | solution.py:893
  519.3 3.7 multiply_subtract_fusion.1
  (269 shorter events, 70.4 us)
Async XLA Ops:
  0.7 18.7 %copy-start.25 = (f32[256,1024]{1,0:T(8,128)S(1)}, f32[256,1024]{1,0:T(8,128)}, u32[]{:S(2)}) copy-start(f32[256,1024]{1,0:T(8,128)} %param.15) | copy-start | bytes 3145732
  5.6 89.3 %collective-permute-start = (bf16[3,1024]{1,0:T(4,128)(2,1)}, bf16[3,1024]{1,0:T(4,128)(2,1)}, u32[]{:S(2)}, u32[]{:S(2)}) collective-permute-start(bf16[3,1024]{1,0:T(4,128)(2,1)} %slice.185), channel_id=1, source_target_pairs={{0,1},{1,2},{2,3},{4,5},{5,6},{6,7},{8,9},{9,10},{10,11},{12,13},{... | collective-permute-start | bytes 18440 | tf_op jit(solution)/shard_map/ppermute | solution.py:37
  9.8 96.2 %copy-start.41 = (f32[4096]{0:T(1024)}, f32[4096]{0:T(1024)S(1)}, u32[]{:S(2)}) copy-start(f32[4096]{0:T(1024)S(1)} %get-tuple-element.100) | copy-start | bytes 49156
  9.8 96.2 %copy-start.43 = (f32[4096]{0:T(1024)}, f32[4096]{0:T(1024)S(1)}, u32[]{:S(2)}) copy-start(f32[4096]{0:T(1024)S(1)} %get-tuple-element.101) | copy-start | bytes 49156
  9.8 96.2 %copy-start.45 = (f32[4096]{0:T(1024)}, f32[4096]{0:T(1024)S(1)}, u32[]{:S(2)}) copy-start(f32[4096]{0:T(1024)S(1)} %get-tuple-element.102) | copy-start | bytes 49156
  9.8 96.2 %copy-start.47 = (f32[4096]{0:T(1024)}, f32[4096]{0:T(1024)S(1)}, u32[]{:S(2)}) copy-start(f32[4096]{0:T(1024)S(1)} %get-tuple-element.103) | copy-start | bytes 49156
  13.5 74.6 %copy-start.76 = (f32[8]{0:T(128)}, f32[8]{0:T(128)S(1)}, u32[]{:S(2)}) copy-start(f32[8]{0:T(128)S(1)} %get-tuple-element.98) | copy-start | bytes 100
  13.5 74.6 %copy-start.78 = (f32[8]{0:T(128)}, f32[8]{0:T(128)S(1)}, u32[]{:S(2)}) copy-start(f32[8]{0:T(128)S(1)} %get-tuple-element.99) | copy-start | bytes 100
  15.4 72.8 %copy-start.52 = (f32[128,16]{0,1:T(8,128)}, f32[128,16]{0,1:T(8,128)S(1)}, u32[]{:S(2)}) copy-start(f32[128,16]{0,1:T(8,128)S(1)} %fusion.60) | copy-start | bytes 24580
  17.8 70.4 %copy-start.65 = (pred[128]{0:T(512)(128)(4,1)}, pred[128]{0:T(512)(128)(4,1)S(1)}, u32[]{:S(2)}) copy-start(pred[128]{0:T(512)(128)(4,1)S(1)} %get-tuple-element.108) | copy-start | bytes 388
  17.8 70.4 %copy-start.71 = (pred[128]{0:T(512)(128)(4,1)}, pred[128]{0:T(512)(128)(4,1)S(1)}, u32[]{:S(2)}) copy-start(pred[128]{0:T(512)(128)(4,1)S(1)} %get-tuple-element.109) | copy-start | bytes 388
  20.2 68.4 %copy-start.56 = (f32[8,1,1,128]{3,0,2,1:T(8,128)S(1)}, f32[8,1,1,128]{3,0,2,1:T(8,128)}, u32[]{:S(2)}) copy-start(f32[8,1,1,128]{3,0,2,1:T(8,128)} %get-tuple-element.107) | copy-start | bytes 12292
  20.2 68.6 %copy-start.55 = (f32[8,1,1,128]{3,0,2,1:T(8,128)S(1)}, f32[8,1,1,128]{3,0,2,1:T(8,128)}, u32[]{:S(2)}) copy-start(f32[8,1,1,128]{3,0,2,1:T(8,128)} %get-tuple-element.106) | copy-start | bytes 12292
  122.0 110.2 %collective-permute-start.5 = (bf16[8,128,256]{2,1,0:T(8,128)(2,1)}, bf16[8,128,256]{2,1,0:T(8,128)(2,1)}, u32[]{:S(2)}, u32[]{:S(2)}) collective-permute-start(bf16[8,128,256]{2,1,0:T(8,128)(2,1)} %convert_bitcast_fusion.1), channel_id=1, source_target_pairs={{0,2},{1,3},{4,6},{5,7},{8,10},{9,11},{12,14},{13,15},{16,18},{17,... | collective-permute-start | bytes 1572872 | tf_op jit(solution)/shard_map/ppermute | solution.py:37
  125.8 107.8 %collective-permute-start.4 = (bf16[8,128,256]{2,1,0:T(8,128)(2,1)}, bf16[8,128,256]{2,1,0:T(8,128)(2,1)}, u32[]{:S(2)}, u32[]{:S(2)}) collective-permute-start(bf16[8,128,256]{2,1,0:T(8,128)(2,1)} %convert_bitcast_fusion.1), channel_id=1, source_target_pairs={{0,3},{4,7},{8,11},{12,15},{16,19},{20,23},{24,27},{28,31}} | collective-permute-start | bytes 1572872 | tf_op jit(solution)/shard_map/ppermute | solution.py:37
  128.1 94.1 %collective-permute-start.2 = (bf16[8,128,128]{2,1,0:T(8,128)(2,1)}, bf16[8,128,128]{2,1,0:T(8,128)(2,1)}, u32[]{:S(2)}, u32[]{:S(2)}) collective-permute-start(bf16[8,128,128]{2,1,0:T(8,128)(2,1)} %convert_bitcast_fusion.2), channel_id=1, source_target_pairs={{0,2},{1,3},{4,6},{5,7},{8,10},{9,11},{12,14},{13,15},{16,18},{17,... | collective-permute-start | bytes 786440 | tf_op jit(solution)/shard_map/ppermute | solution.py:37
  130.1 100.8 %collective-permute-start.3 = (bf16[8,128,128]{2,1,0:T(8,128)(2,1)}, bf16[8,128,128]{2,1,0:T(8,128)(2,1)}, u32[]{:S(2)}, u32[]{:S(2)}) collective-permute-start(bf16[8,128,128]{2,1,0:T(8,128)(2,1)} %convert_bitcast_fusion.2), channel_id=1, source_target_pairs={{0,3},{4,7},{8,11},{12,15},{16,19},{20,23},{24,27},{28,31}} | collective-permute-start | bytes 786440 | tf_op jit(solution)/shard_map/ppermute | solution.py:37
  131.5 105.9 %collective-permute-start.6 = (bf16[8,128,256]{2,1,0:T(8,128)(2,1)}, bf16[8,128,256]{2,1,0:T(8,128)(2,1)}, u32[]{:S(2)}, u32[]{:S(2)}) collective-permute-start(bf16[8,128,256]{2,1,0:T(8,128)(2,1)} %convert_bitcast_fusion.1), channel_id=1, source_target_pairs={{0,1},{1,2},{2,3},{4,5},{5,6},{6,7},{8,9},{9,10},{10,11},{12,13},{... | collective-permute-start | bytes 1572872 | tf_op jit(solution)/shard_map/ppermute | solution.py:37
  134.5 85.6 %copy-start.29 = (f32[1,128,1024]{2,1,0:T(8,128)S(1)}, f32[1,128,1024]{2,1,0:T(8,128)}, u32[]{:S(2)}) copy-start(f32[1,128,1024]{2,1,0:T(8,128)} %param.14) | copy-start | bytes 1572868
  222.2 15.1 %collective-permute-start.1 = (bf16[8,128,128]{2,1,0:T(8,128)(2,1)}, bf16[8,128,128]{2,1,0:T(8,128)(2,1)}, u32[]{:S(2)}, u32[]{:S(2)}) collective-permute-start(bf16[8,128,128]{2,1,0:T(8,128)(2,1)} %convert_bitcast_fusion.2), channel_id=1, source_target_pairs={{0,1},{1,2},{2,3},{4,5},{5,6},{6,7},{8,9},{9,10},{10,11},{12,13},{... | collective-permute-start | bytes 786440 | tf_op jit(solution)/shard_map/ppermute | solution.py:37
  230.9 154.0 %collective-permute-start.8 = (bf16[8,128,128]{2,1,0:T(8,128)(2,1)}, bf16[8,128,128]{2,1,0:T(8,128)(2,1)}, u32[]{:S(2)}, u32[]{:S(2)}) collective-permute-start(bf16[8,128,128]{2,1,0:T(8,128)(2,1)} %convert_bitcast_fusion.2), channel_id=1, source_target_pairs={{2,0},{3,1},{6,4},{7,5},{10,8},{11,9},{14,12},{15,13},{18,16},{19,... | collective-permute-start | bytes 786440 | tf_op jit(solution)/shard_map/ppermute | solution.py:37
  232.3 155.0 %collective-permute-start.9 = (bf16[8,128,128]{2,1,0:T(8,128)(2,1)}, bf16[8,128,128]{2,1,0:T(8,128)(2,1)}, u32[]{:S(2)}, u32[]{:S(2)}) collective-permute-start(bf16[8,128,128]{2,1,0:T(8,128)(2,1)} %convert_bitcast_fusion.2), channel_id=1, source_target_pairs={{3,0},{7,4},{11,8},{15,12},{19,16},{23,20},{27,24},{31,28}} | collective-permute-start | bytes 786440 | tf_op jit(solution)/shard_map/ppermute | solution.py:37
  271.0 116.2 %collective-permute-start.11 = (bf16[8,128,256]{2,1,0:T(8,128)(2,1)}, bf16[8,128,256]{2,1,0:T(8,128)(2,1)}, u32[]{:S(2)}, u32[]{:S(2)}) collective-permute-start(bf16[8,128,256]{2,1,0:T(8,128)(2,1)} %convert_bitcast_fusion), channel_id=1, source_target_pairs={{2,0},{3,1},{6,4},{7,5},{10,8},{11,9},{14,12},{15,13},{18,16},{19,... | collective-permute-start | bytes 1572872 | tf_op jit(solution)/shard_map/ppermute | solution.py:37
  272.3 114.9 %collective-permute-start.10 = (bf16[8,128,256]{2,1,0:T(8,128)(2,1)}, bf16[8,128,256]{2,1,0:T(8,128)(2,1)}, u32[]{:S(2)}, u32[]{:S(2)}) collective-permute-start(bf16[8,128,256]{2,1,0:T(8,128)(2,1)} %convert_bitcast_fusion), channel_id=1, source_target_pairs={{3,0},{7,4},{11,8},{15,12},{19,16},{23,20},{27,24},{31,28}} | collective-permute-start | bytes 1572872 | tf_op jit(solution)/shard_map/ppermute | solution.py:37
  273.8 120.7 %collective-permute-start.12 = (bf16[8,128,256]{2,1,0:T(8,128)(2,1)}, bf16[8,128,256]{2,1,0:T(8,128)(2,1)}, u32[]{:S(2)}, u32[]{:S(2)}) collective-permute-start(bf16[8,128,256]{2,1,0:T(8,128)(2,1)} %convert_bitcast_fusion), channel_id=1, source_target_pairs={{1,0},{2,1},{3,2},{5,4},{6,5},{7,6},{9,8},{10,9},{11,10},{13,12},{... | collective-permute-start | bytes 1572872 | tf_op jit(solution)/shard_map/ppermute | solution.py:37
  286.6 92.4 %copy-start.32 = (f32[264,1024]{1,0:T(8,128)S(1)}, f32[264,1024]{1,0:T(8,128)}, u32[]{:S(2)}) copy-start(f32[264,1024]{1,0:T(8,128)} %param.19) | copy-start | bytes 3244036
  286.6 92.4 %copy-start.33 = (f32[264,1024]{1,0:T(8,128)S(1)}, f32[264,1024]{1,0:T(8,128)}, u32[]{:S(2)}) copy-start(f32[264,1024]{1,0:T(8,128)} %param.20) | copy-start | bytes 3244036
  385.0 9.5 %collective-permute-start.7 = (bf16[8,128,128]{2,1,0:T(8,128)(2,1)}, bf16[8,128,128]{2,1,0:T(8,128)(2,1)S(1)}, u32[]{:S(2)}, u32[]{:S(2)}) collective-permute-start(bf16[8,128,128]{2,1,0:T(8,128)(2,1)} %convert_bitcast_fusion.2), channel_id=1, source_target_pairs={{1,0},{2,1},{3,2},{5,4},{6,5},{7,6},{9,8},{10,9},{11,10},{13,12},{... | collective-permute-start | bytes 786440 | tf_op jit(solution)/shard_map/ppermute | solution.py:37
  418.6 7.0 %collective-permute-start.13 = (bf16[3,4096]{1,0:T(4,128)(2,1)S(1)}, bf16[3,4096]{1,0:T(4,128)(2,1)S(1)}, u32[]{:S(2)}, u32[]{:S(2)}) collective-permute-start(bf16[3,4096]{1,0:T(4,128)(2,1)S(1)} %slice.201), channel_id=1, source_target_pairs={{1,0},{2,1},{3,2},{5,4},{6,5},{7,6},{9,8},{10,9},{11,10},{13,12},{... | collective-permute-start | bytes 73736 | tf_op jit(solution)/shard_map/ppermute | solution.py:37
  431.2 88.0 %copy-start.26 = (f32[256,1024]{1,0:T(8,128)S(1)}, f32[256,1024]{1,0:T(8,128)}, u32[]{:S(2)}) copy-start(f32[256,1024]{1,0:T(8,128)} %param.15) | copy-start | bytes 3145732
  431.3 87.9 %copy-start.34 = (f32[256,1024]{1,0:T(8,128)S(1)}, f32[256,1024]{1,0:T(8,128)}, u32[]{:S(2)}) copy-start(f32[256,1024]{1,0:T(8,128)} %param.16) | copy-start | bytes 3145732
  431.3 87.9 %copy-start.35 = (f32[256,1024]{1,0:T(8,128)S(1)}, f32[256,1024]{1,0:T(8,128)}, u32[]{:S(2)}) copy-start(f32[256,1024]{1,0:T(8,128)} %param.17) | copy-start | bytes 3145732
  (66 other events, 276.5 us)
